TPU v7x, 32 devices: a whole 2x2x4 slice. The times are simulated.
32 devices in a mesh: dp: 16 (over z, y, x), tensor: 2 (over core).
Axes of the slice: x: 2, y: 2, z: 4, core: 2. Of those that a mesh axis runs over, the one named last changes fastest.
Arguments:
- pool: bfloat16 [4096, 2048], P('dp', 'tensor'), may hold values from -6 to 6
- select: int32 [2048], P('dp'), may hold values from 0 to 4095, as said below
- reward_w: bfloat16 [2048], P('tensor'), may hold values from -0.125 to 0.125
- routes: int32 [2048, 6], P('dp'), may hold values from 0 to 15, all different within a row; in each aligned block of 128 rows (0 to 127, 128 to 255, ...) at most 60 rows name the same one
- gates: float32 [2048, 6], P('dp'), may hold values from 0.05 to 0.5
- target: bfloat16 [2048, 2048], P('dp', 'tensor'), may hold values from -6 to 6
- w_gate: bfloat16 [16, 1408, 2048], P('dp', 'tensor'), may hold values from -0.125 to 0.125
- w_up: bfloat16 [16, 1408, 2048], P('dp', 'tensor'), may hold values from -0.125 to 0.125
- w_down: bfloat16 [16, 1408, 2048], P('dp', 'tensor'), may hold values from -0.15625 to 0.15625
Outputs:
- mixed: bfloat16 [2048, 2048], P('dp', 'tensor')
- grad_gate: bfloat16 [16, 1408, 2048], P('dp', 'tensor')
- grad_up: bfloat16 [16, 1408, 2048], P('dp', 'tensor')
- grad_down: bfloat16 [16, 1408, 2048], P('dp', 'tensor')
Inputs may be any that keep to these rules, and one draw needn't show every extreme that they name: The 128 entries of aligned block i of select are distinct rows of pool's block i, rows i * 256 to (i + 1) * 256 - 1. `routes`: each row names 6 different experts. In the 128 rows of one device no expert is named more than 60 times, a bound that some block reaches.
All inputs are finite; a program needn't handle non-finite values.
Results may differ from a plain program's by a relative error of at most 0.015.
Values may be sent and summed in bfloat16 or wider, within the bound.
A program may use at most 128 MiB of HBM per device.

v0:
```python
import functools
import jax
import jax.numpy as jnp
from jax import lax
from jax.experimental import pallas as pl
from jax.experimental.pallas import tpu as pltpu
from jax.sharding import PartitionSpec as P

MESH = pl.DeviceIdType.MESH
PLANE = 4
F32 = jnp.float32
BF16 = jnp.bfloat16


def slot_factor(route_hit, weights):
    return jnp.sum(jnp.where(route_hit, weights.reshape(-1)[:, None], 0.0), axis=0)


def generic(pool, select, reward_w, routes, gates, target, w_gate, w_up, w_down):
    pool_rows = pool.shape[0]
    local_rows = select - lax.axis_index("dp") * pool_rows
    chosen = jnp.take(pool, local_rows, axis=0)
    sel_rows, top_count = routes.shape
    owners = lax.axis_size("dp")
    exp_dev = w_gate.shape[0]
    experts = owners * exp_dev
    capacity = 5 * sel_rows * top_count // (4 * experts)
    slot_count = experts * capacity
    flat_routes = routes.reshape(-1)
    onehot = (flat_routes[:, None] == jnp.arange(experts, dtype=jnp.int32)[None, :]).astype(
        jnp.int32
    )
    before = jnp.cumsum(onehot, axis=0) - onehot
    slot_rank = jnp.sum(before * onehot, axis=1)
    slot_place = flat_routes * capacity + slot_rank
    route_hit = slot_place[:, None] == jnp.arange(slot_count, dtype=jnp.int32)[None, :]
    route_pick = route_hit.astype(jnp.bfloat16).reshape(sel_rows, top_count, slot_count)
    token_pick = jnp.sum(route_pick, axis=1)
    reward = lax.psum(jnp.dot(chosen, reward_w, preferred_element_type=jnp.float32), "tensor")
    keep_scale = jax.nn.sigmoid(reward)
    slot_scale = slot_factor(route_hit, keep_scale[:, None] * gates)
    token_send = jnp.einsum(
        "sp,sd->pd", token_pick, chosen, preferred_element_type=jnp.float32
    ).astype(jnp.bfloat16)
    picked_target = jnp.einsum("sp,sd->pd", token_pick, target, preferred_element_type=jnp.float32)
    cot_send = (picked_target * slot_scale[:, None]).astype(jnp.bfloat16)
    token_part, cot_part = (
        lax.all_to_all(token_send, "dp", split_axis=0, concat_axis=0, tiled=True),
        lax.all_to_all(cot_send, "dp", split_axis=0, concat_axis=0, tiled=True),
    )
    received_tokens, received_cots = (
        lax.all_gather(token_part, "tensor", axis=1, tiled=True),
        lax.all_gather(cot_part, "tensor", axis=1, tiled=True),
    )
    width = received_tokens.shape[1]
    token_rows = received_tokens.reshape(owners, exp_dev, capacity, width)
    cot_rows = received_cots.reshape(owners, exp_dev, capacity, width)
    gate_act = jnp.einsum("secd,efd->secf", token_rows, w_gate, preferred_element_type=jnp.float32)
    up_act = jnp.einsum("secd,efd->secf", token_rows, w_up, preferred_element_type=jnp.float32)
    sigmoid_gate = jax.nn.sigmoid(gate_act)
    hidden = (gate_act * sigmoid_gate * up_act).astype(jnp.bfloat16)
    partial_value = jnp.einsum("secf,efd->secd", hidden, w_down, preferred_element_type=jnp.float32)
    summed = lax.psum_scatter(
        partial_value.astype(jnp.bfloat16), "tensor", scatter_dimension=3, tiled=True
    )
    returned = lax.all_to_all(summed, "dp", split_axis=0, concat_axis=0, tiled=True).reshape(
        slot_count, -1
    )
    route_rows = jnp.einsum("skp,pd->skd", route_pick, returned, preferred_element_type=jnp.float32)
    mixed = jnp.sum(route_rows * gates[:, :, None], axis=1).astype(jnp.bfloat16)
    hidden_grad = jnp.einsum("secd,efd->secf", cot_rows, w_down, preferred_element_type=jnp.float32)
    gate_grad = (
        hidden_grad * up_act * sigmoid_gate * (1.0 + gate_act * (1.0 - sigmoid_gate))
    ).astype(jnp.bfloat16)
    up_grad = (hidden_grad * gate_act * sigmoid_gate).astype(jnp.bfloat16)
    grad_down = jnp.einsum(
        "secf,secd->efd", hidden, cot_rows, preferred_element_type=jnp.float32
    ).astype(jnp.bfloat16)
    grad_gate = jnp.einsum(
        "secf,secd->efd", gate_grad, token_rows, preferred_element_type=jnp.float32
    ).astype(jnp.bfloat16)
    grad_up = jnp.einsum(
        "secf,secd->efd", up_grad, token_rows, preferred_element_type=jnp.float32
    ).astype(jnp.bfloat16)
    return (mixed, grad_gate, grad_up, grad_down)


def place(line):
    d = lax.axis_index("dp")
    c = lax.axis_index("tensor")
    z, q = d // PLANE, d % PLANE
    y, x = q // 2, q % 2
    mates = [((y + ry) % 2) * 2 + (x + rx) % 2 for ry, rx in ((0, 1), (1, 0), (1, 1))]
    return d, c, z, q, mates


def greet(d, c, z, q, mates, line):
    barrier = pltpu.get_barrier_semaphore()
    for m in mates:
        pl.semaphore_signal(barrier, inc=1, device_id=(z * PLANE + m, c), device_id_type=MESH)
    pl.semaphore_signal(barrier, inc=1, device_id=(d, 1 - c), device_id_type=MESH)

    @pl.when(z > 0)
    def _():
        pl.semaphore_signal(barrier, inc=1, device_id=(d - PLANE, c), device_id_type=MESH)

    @pl.when(z < line - 1)
    def _():
        pl.semaphore_signal(barrier, inc=1, device_id=(d + PLANE, c), device_id_type=MESH)


def greeted(z, line):
    below, above = (z + line - 1) // line, (2 * line - 2 - z) // line
    pl.semaphore_wait(pltpu.get_barrier_semaphore(), 4 + below + above)


def remote(src, dst, send, recv, dev):
    return pltpu.make_async_remote_copy(
        src_ref=src, dst_ref=dst, send_sem=send, recv_sem=recv, device_id=dev, device_id_type=MESH
    )


def layer_kernel(
    line, pad, pool_hbm, sel_ref, rw_ref, rt_ref, gt_ref, target_hbm, wg_hbm, wu_hbm, wd_hbm,
    mixed_ref, gg_ref, gu_ref, gd_ref,
    pool_ref, rt_vmem, gt_vmem, tok, cot, gate_act, up_act, hid, ggrad, ugrad, val,
    data, side_ref, scale, part, part_in, stage,
    partner_in, back, plane_in, acc, out_stage, line_in,
    lsem, zsend, zrecv, ssend, srecv, csend, crecv, xsend, xrecv, tsend, trecv, psend, precv,
    vsend, vrecv, bsend, brecv, usend, urecv,
):
    d, c, z, q, mates = place(line)
    experts = line * PLANE
    sel_rows, half = mixed_ref.shape
    top = gt_ref.shape[0]
    wg, wu, wd = gg_ref.at[0], gu_ref.at[0], gd_ref.at[0]
    units, width = wg.shape
    span = PLANE * pad
    rows = (tok, cot)
    mine = pl.ds(pl.multiple_of(c * half, half), half)
    other = pl.ds(pl.multiple_of((1 - c) * half, half), half)
    partner = (d, 1 - c)
    turn = 2 * (z // (line // 2)) - 1

    def order(i):
        return (z + turn * (1 + i) + 2 * line) % line

    greet(d, c, z, q, mates, line)
    loads = [
        pltpu.make_async_copy(src, dst, lsem.at[i])
        for i, (src, dst) in enumerate((
            (pool_hbm, pool_ref), (target_hbm, data.at[1, z]), (wg_hbm.at[0], wg),
            (wu_hbm.at[0], wu), (wd_hbm.at[0], wd), (rt_ref, rt_vmem), (gt_ref, gt_vmem),
        ))
    ]
    for i in (5, 6, 0, 1, 2, 3, 4):
        loads[i].start()

    loads[5].wait()
    loads[6].wait()
    expert_id = lax.broadcasted_iota(jnp.int32, (experts, sel_rows), 0)
    member = jnp.zeros((experts, sel_rows), F32)
    gate = jnp.zeros((experts, sel_rows), F32)
    for k in range(top):
        eq = rt_vmem[k : k + 1, :] == expert_id
        member = member + jnp.where(eq, 1.0, 0.0)
        gate = gate + jnp.where(eq, gt_vmem[k : k + 1, :], 0.0)
    tri = jnp.where(
        lax.broadcasted_iota(jnp.int32, (sel_rows, sel_rows), 0)
        < lax.broadcasted_iota(jnp.int32, (sel_rows, sel_rows), 1),
        1.0,
        0.0,
    ).astype(BF16)
    before = jnp.dot(member.astype(BF16), tri, preferred_element_type=F32)
    side_ref[z, 0:experts, :] = jnp.where(member > 0.5, before, -1.0)
    side_ref[z, experts : 2 * experts, :] = gate

    pool_rows = pool_ref.shape[0]
    hit = (
        lax.broadcasted_iota(jnp.int32, (pool_rows, sel_rows), 0) == sel_ref[...] - d * pool_rows
    ).astype(F32).astype(BF16)
    loads[0].wait()
    chosen = lax.dot_general(
        hit, pool_ref[...], (((0,), (0,)), ((), ())), preferred_element_type=F32
    ).astype(BF16)
    data[0, z] = chosen
    part[...] = lax.dot_general(
        rw_ref[...], chosen,
        (((1,), (1,)), ((), ())), preferred_element_type=F32,
    )

    greeted(z, line)
    reward_copy = remote(part, part_in, psend, precv, partner)
    reward_copy.start()

    def zcopies(a, s, way):
        blk = z - way * s
        dev = (d + way * PLANE, c)
        w = (way + 1) // 2
        main = remote(data.at[a, blk], data.at[a, blk], zsend.at[a, w, s], zrecv.at[a, blk], dev)
        if a == 0:
            extra = remote(
                side_ref.at[blk], side_ref.at[blk], ssend.at[w, s], srecv.at[blk], dev
            )
        else:
            extra = remote(scale.at[blk], scale.at[blk], csend.at[w, s], crecv.at[blk], dev)
        return extra, main

    def sends(a, s, way):
        blk, to = z - way * s, z + way
        return (blk >= 0) & (blk < line) & (to >= 0) & (to < line)

    def zstart(a, s):
        for way in (1, -1):
            @pl.when(sends(a, s, way))
            def _():
                for cp in zcopies(a, s, way):
                    cp.start()

    def arrives(s, way):
        blk = z - way * (s + 1)
        return (blk >= 0) & (blk < line)

    def zwait(a, s):
        for way in (1, -1):
            @pl.when(arrives(s, way))
            def _():
                blk = z - way * (s + 1)
                remote(
                    data.at[a, blk], data.at[a, blk], zsend.at[a, 0, 0], zrecv.at[a, blk], partner
                ).wait_recv()
                if a == 0:
                    remote(
                        side_ref.at[blk], side_ref.at[blk], ssend.at[0, 0], srecv.at[blk], partner
                    ).wait_recv()
                else:
                    remote(
                        scale.at[blk], scale.at[blk], csend.at[0, 0], crecv.at[blk], partner
                    ).wait_recv()

    def tcopy(a, b):
        spot = rows[a].at[b, :, mine]
        return remote(spot, spot, tsend.at[a, b], trecv.at[a, b], partner)

    def tarrive(a, b):
        spot = rows[a].at[b, :, other]
        remote(spot, spot, tsend.at[a, b], trecv.at[a, b], partner).wait_recv()

    def xcopy(a, zp, r):
        return remote(
            stage.at[a, zp, r],
            rows[a].at[zp * PLANE + q, :, mine],
            xsend.at[a, zp, r],
            xrecv.at[a, zp * PLANE + q],
            (z * PLANE + mates[r], c),
        )

    slot_id = lax.broadcasted_iota(jnp.int32, (pad, sel_rows), 0).astype(F32)

    def process(a, zp):
        block = data[a, zp]
        for r in (2, 0, 1, 3):
            e = z * PLANE + (mates[r] if r < 3 else q)
            m = slot_id == side_ref[zp, pl.ds(e, 1), :]
            picked = jnp.dot(
                jnp.where(m, 1.0, 0.0).astype(BF16), block, preferred_element_type=F32
            )
            if a == 1:
                picked = picked * jnp.sum(
                    jnp.where(m, scale[zp, pl.ds(e, 1), :], 0.0), axis=1, keepdims=True
                )
            picked = picked.astype(BF16)
            if r < 3:
                stage[a, zp, r] = picked
                xcopy(a, zp, r).start()
            else:
                rows[a][zp * PLANE + q, :, mine] = picked
                tcopy(a, zp * PLANE + q).start()

    def forward(a, zp):
        for r in range(3):
            b = zp * PLANE + mates[r]
            remote(
                stage.at[a, zp, r], rows[a].at[b, :, mine], xsend.at[a, zp, r],
                xrecv.at[a, b], partner,
            ).wait_recv()
            tcopy(a, b).start()

    def got(fn, a, s):
        for way in (1, -1):
            @pl.when(arrives(s, way))
            def _():
                fn(a, z - way * (s + 1))

    def vcopy(b):
        return remote(val.at[b, :, other], partner_in.at[b], vsend.at[b], vrecv.at[b], partner)

    def lanes(zp):
        return pl.ds(pl.multiple_of(zp * span, span), span)

    def sigmoid(v):
        return 1.0 / (1.0 + jnp.exp(-v))

    nt = (((1,), (1,)), ((), ()))
    tn = (((0,), (0,)), ((), ()))
    tile = 512 if width % 512 == 0 else width

    def group(zp):
        for j in range(PLANE):
            tarrive(0, zp * PLANE + j)
        x = tok[pl.ds(zp * PLANE, PLANE)].reshape(span, width)
        g = lax.dot_general(wg[...], x, nt, preferred_element_type=F32)
        u = lax.dot_general(wu[...], x, nt, preferred_element_type=F32)
        gate_act[zp] = g
        up_act[zp] = u
        h = (g * sigmoid(g) * u).astype(BF16)
        hid[:, lanes(zp)] = h
        for n in range(width // tile):
            cols = pl.ds(n * tile, tile)
            v = lax.dot_general(h, wd[:, cols], tn, preferred_element_type=F32)
            val[pl.ds(zp * PLANE, PLANE), :, cols] = v.astype(BF16).reshape(PLANE, pad, tile)
        for j in range(PLANE):
            vcopy(zp * PLANE + j).start()

    def grad_group(zp):
        for j in range(PLANE):
            tarrive(1, zp * PLANE + j)
        x = cot[pl.ds(zp * PLANE, PLANE)].reshape(span, width)
        hg = lax.dot_general(wd[...], x, nt, preferred_element_type=F32)
        g = gate_act[zp]
        s = sigmoid(g)
        ggrad[:, lanes(zp)] = (hg * up_act[zp] * s * (1.0 + g * (1.0 - s))).astype(BF16)
        ugrad[:, lanes(zp)] = (hg * g * s).astype(BF16)

    grads = ((ggrad, tok, wg), (ugrad, tok, wu), (hid, cot, wd))
    strip = 256 if width % 256 == 0 else width
    strips = width // strip

    def grad_strip(n, carry):
        cols = pl.ds(pl.multiple_of(n * strip, strip), strip)
        for left, right, out in grads:
            r = right[:, :, cols].reshape(experts * pad, strip)
            out[:, cols] = jnp.dot(left[...], r, preferred_element_type=F32).astype(BF16)
        return carry

    def bcopy(zp, r):
        return remote(
            back.at[zp, r], plane_in.at[zp, q], bsend.at[zp, r], brecv.at[zp, q],
            (z * PLANE + mates[r], c),
        )

    def give(zp):
        for r in (2, 0, 1, 3):
            b = zp * PLANE + (mates[r] if r < 3 else q)
            vcopy(b).wait_recv()
            total = (val[b, :, mine].astype(F32) + partner_in[b].astype(F32)).astype(BF16)
            if r < 3:
                back[zp, r] = total
                bcopy(zp, r).start()
            else:
                plane_in[zp, q] = total

    def combine(zp):
        for r in range(3):
            remote(
                back.at[zp, r], plane_in.at[zp, mates[r]], bsend.at[zp, r],
                brecv.at[zp, mates[r]], partner,
            ).wait_recv()
        total = jnp.zeros((sel_rows, half), F32)
        for j in range(PLANE):
            e = z * PLANE + j
            w = jnp.where(
                slot_id == side_ref[zp, pl.ds(e, 1), :],
                side_ref[zp, pl.ds(experts + e, 1), :],
                0.0,
            )
            high = w.astype(BF16)
            low = (w - high.astype(F32)).astype(BF16)
            both = jnp.concatenate([high, low], axis=0)
            values = plane_in[zp, j]
            total = total + lax.dot_general(
                both, jnp.concatenate([values, values], axis=0), tn, preferred_element_type=F32
            )
        acc[zp] = total

    def ucopy(w, s):
        to = d + (2 * w - 1) * PLANE
        return remote(
            out_stage.at[w, s], line_in.at[w, s], usend.at[w, s], urecv.at[w, s], (to, c)
        )

    def height(w):
        return z if w == 1 else line - 1 - z

    def lifts(w, s):
        return (height(w) <= s) & (height(w) < line - 1)

    def lands(w, s):
        return (height(w) > 0) & (height(w) - 1 <= s)

    zstart(0, 0)
    process(0, z)
    reward_copy.wait()
    scale[z] = sigmoid(part[0:1, :] + part_in[0:1, :]) * side_ref[z, experts : 2 * experts, :]
    last = line - 2
    for a in (0, 1):
        for s in range(line - 1):
            zwait(a, s)
            if s < last:
                zstart(a, s + 1)
            elif a == 0:
                loads[1].wait()
                zstart(1, 0)
            got(process, a, s)
            if s == 0:
                forward(a, z)
            else:
                got(forward, a, s - 1)
            if a == 1:
                if s == last:
                    for i in range(line - 1):
                        give(order(i))
                    group(order(line - 1))
                else:
                    group(order(s + 1))
        if a == 0:
            process(1, z)
        got(forward, a, last)
        if a == 0:
            for cp in loads[2:5]:
                cp.wait()
            group(order(0))
    give(z)

    for i in range(line):
        grad_group(order(line - 1 - i))
    done = 0
    for s in range(line - 1):
        combine(order(s))
        if s > 0:
            for w in (1, 0):
                @pl.when(lands(w, s - 1))
                def _():
                    ucopy(w, s - 1).wait_recv()
        for w in (1, 0):
            blk = z + (2 * w - 1) * (line - 1 - s)

            @pl.when(lifts(w, s) & (height(w) > 0))
            def _():
                if s > 0:
                    out_stage[w, s] = (acc[blk] + line_in[w, s - 1].astype(F32)).astype(BF16)
                    ucopy(w, s).start()

            @pl.when(lifts(w, s) & (height(w) == 0))
            def _():
                out_stage[w, s] = acc[blk].astype(BF16)
                ucopy(w, s).start()
        upto = strips * (s + 1) // line
        lax.fori_loop(done, upto, grad_strip, 0)
        done = upto
    combine(z)
    lax.fori_loop(done, strips, grad_strip, 0)
    for w in (1, 0):
        @pl.when(lands(w, last))
        def _():
            ucopy(w, last).wait_recv()
            acc[z] = acc[z] + line_in[w, last].astype(F32)
    mixed_ref[...] = acc[z].astype(BF16)

    for b in range(experts):
        vcopy(b).wait_send()
        for a in (0, 1):
            tcopy(a, b).wait_send()
    for zp in range(line):
        for r in range(3):
            bcopy(zp, r).wait_send()
            for a in (0, 1):
                xcopy(a, zp, r).wait_send()
    for s in range(line - 1):
        for w in (1, 0):
            @pl.when(lifts(w, s))
            def _():
                ucopy(w, s).wait_send()

        for a in (0, 1):
            for way in (1, -1):
                @pl.when(sends(a, s, way))
                def _():
                    for cp in zcopies(a, s, way):
                        cp.wait_send()


def vmem(count):
    return [pl.BlockSpec(memory_space=pltpu.VMEM)] * count


def hbm(count):
    return [pl.BlockSpec(memory_space=pl.ANY)] * count


DMA = pltpu.SemaphoreType.DMA


def planar(pool, select, reward_w, routes, gates, target, w_gate, w_up, w_down):
    dp = lax.axis_size("dp")
    line = dp // PLANE
    experts = dp * w_gate.shape[0]
    sel_rows, top = routes.shape
    capacity = 5 * sel_rows * top // (4 * experts)
    pad = -(-capacity // 16) * 16
    half = target.shape[1]
    units, width = w_gate.shape[1:]
    span = PLANE * pad
    grad_shape = pltpu.VMEM(w_gate.shape, BF16)
    rw = jnp.broadcast_to(reward_w[None, :], (16, half))
    slots = pltpu.VMEM((experts, pad, width), BF16)
    act = pltpu.VMEM((line, units, span), F32)
    flat = pltpu.VMEM((units, experts * pad), BF16)
    return pl.pallas_call(
        functools.partial(layer_kernel, line, pad),
        name="layer",
        out_shape=(pltpu.VMEM((sel_rows, half), BF16), grad_shape, grad_shape, grad_shape),
        in_specs=hbm(1) + vmem(2) + hbm(6),
        out_specs=tuple(vmem(4)),
        scratch_shapes=[
            pltpu.VMEM(pool.shape, BF16), pltpu.VMEM((top, sel_rows), jnp.int32),
            pltpu.VMEM((top, sel_rows), F32), slots, slots, act, act, flat, flat, flat, slots,
            pltpu.VMEM((2, line, sel_rows, half), BF16),
            pltpu.VMEM((line, 2 * experts, sel_rows), F32),
            pltpu.VMEM((line, experts, sel_rows), F32),
            pltpu.VMEM((16, sel_rows), F32),
            pltpu.VMEM((16, sel_rows), F32),
            pltpu.VMEM((2, line, 3, pad, half), BF16),
            pltpu.VMEM((experts, pad, half), BF16),
            pltpu.VMEM((line, 3, pad, half), BF16),
            pltpu.VMEM((line, PLANE, pad, half), BF16),
            pltpu.VMEM((line, sel_rows, half), F32),
            pltpu.VMEM((2, line - 1, sel_rows, half), BF16),
            pltpu.VMEM((2, line - 1, sel_rows, half), BF16),
            DMA((7,)),
            DMA((2, 2, line)), DMA((2, line)), DMA((2, line)), DMA((line,)),
            DMA((2, line)), DMA((line,)), DMA((2, line, 3)), DMA((2, experts)),
            DMA((2, experts)), DMA((2, experts)), DMA, DMA,
            DMA((experts,)), DMA((experts,)), DMA((line, 3)), DMA((line, PLANE)),
            DMA((2, line)), DMA((2, line)),
        ],
        compiler_params=pltpu.CompilerParams(
            collective_id=0, has_side_effects=True, vmem_limit_bytes=57 * 10**6
        ),
    )(pool, select.reshape(1, sel_rows), rw, routes.T, gates.T, target,
      w_gate, w_up, w_down)


def solution(mesh):
    in_specs = (
        P("dp", "tensor"), P("dp"), P("tensor"), P("dp", None), P("dp", None), P("dp", "tensor"),
        P("dp", "tensor", None), P("dp", "tensor", None), P("dp", "tensor", None),
    )
    out_specs = (
        P("dp", "tensor"), P("dp", "tensor", None), P("dp", "tensor", None),
        P("dp", "tensor", None),
    )
    dp, tensor = mesh.shape["dp"], mesh.shape["tensor"]
    fits = tensor == 2 and dp % (2 * PLANE) == 0
    local = planar if fits else generic
    return jax.shard_map(local, mesh=mesh, in_specs=in_specs, out_specs=out_specs, check_vma=False)
```

profile of v0, /device:TPU:0, one launch (start us, length us, event | category | flops | bytes accessed | tf_op | source)
XLA Modules:
  0.0 100.2 jit_solution(1681344042717485046)
XLA Ops:
  0.6 1.3 %broadcast_in_dim.2.rw_ref = bf16[16,1024]{1,0:T(8,128)(2,1)} broadcast(bf16[1024]{0:T(1024)(128)(2,1)} %param.11), dimensions={1} | broadcast | bytes 34816 | tf_op jit(solution)/shard_map/broadcast_in_dim | solution.py:515
  1.9 92.8 %layer.1 = (bf16[128,1024]{1,0:T(8,128)(2,1)S(1)}, bf16[1,704,2048]{2,1,0:T(8,128)(2,1)S(1)}, bf16[1,704,2048]{2,1,0:T(8,128)(2,1)S(1)}, bf16[1,704,2048]{2,1,0:T(8,128)(2,1)S(1)}) custom-call(bf16[256,1024]{1,0:T(8,128)(2,1)} %pool_hbm.1, s32[1,128]{1,0:T(1,128)} %bitcast.5, bf16[16,1024]{1,0:T(8,128)(2,1)} %broadcast_in_dim.2.rw_ref, s32[6,128]{1,0:T(8,128)} %bitcast.3, ...), custom_call_target="tpu_custom_call" | custom-call | tf_op jit(solution)/shard_map/layer/pallas_call | solution.py:519
  94.8 0.7 copy.17
  95.5 1.6 %copy.18 = bf16[1,704,2048]{2,1,0:T(8,128)(2,1)} copy(bf16[1,704,2048]{2,1,0:T(8,128)(2,1)S(1)} %get-tuple-element.5) | data formatting | bytes 5767168
  97.0 1.6 %copy.19 = bf16[1,704,2048]{2,1,0:T(8,128)(2,1)} copy(bf16[1,704,2048]{2,1,0:T(8,128)(2,1)S(1)} %get-tuple-element.6) | data formatting | bytes 5767168
  98.6 1.6 %copy.20 = bf16[1,704,2048]{2,1,0:T(8,128)(2,1)} copy(bf16[1,704,2048]{2,1,0:T(8,128)(2,1)S(1)} %get-tuple-element.7) | data formatting | bytes 5767168
where the time goes:
time: 100 us
  Pallas kernels  92.8 us (93%)
  local copies, waits for them, and re-layouts  6.74 us (7%)
    pallas_call x1, Pallas kernels, planar(): pl.pallas_call(functools.partial(layer_kernel, line, pad), name='layer',...  92.8 us
    unnamed x4, local copies, waits for them, and re-layouts  5.44 us

commit v1 on v0

v1 whole, which is shorter than its diff:
```python
import functools
import jax
import jax.numpy as jnp
from jax import lax
from jax.experimental import pallas as pl
from jax.experimental.pallas import tpu as pltpu
from jax.sharding import PartitionSpec as P

MESH = pl.DeviceIdType.MESH
PLANE = 4
LINE = 4
PARTS = 2
F32 = jnp.float32
BF16 = jnp.bfloat16


def slot_factor(route_hit, weights):
    return jnp.sum(jnp.where(route_hit, weights.reshape(-1)[:, None], 0.0), axis=0)


def generic(pool, select, reward_w, routes, gates, target, w_gate, w_up, w_down):
    pool_rows = pool.shape[0]
    local_rows = select - lax.axis_index("dp") * pool_rows
    chosen = jnp.take(pool, local_rows, axis=0)
    sel_rows, top_count = routes.shape
    owners = lax.axis_size("dp")
    exp_dev = w_gate.shape[0]
    experts = owners * exp_dev
    capacity = 5 * sel_rows * top_count // (4 * experts)
    slot_count = experts * capacity
    flat_routes = routes.reshape(-1)
    onehot = (flat_routes[:, None] == jnp.arange(experts, dtype=jnp.int32)[None, :]).astype(
        jnp.int32
    )
    before = jnp.cumsum(onehot, axis=0) - onehot
    slot_rank = jnp.sum(before * onehot, axis=1)
    slot_place = flat_routes * capacity + slot_rank
    route_hit = slot_place[:, None] == jnp.arange(slot_count, dtype=jnp.int32)[None, :]
    route_pick = route_hit.astype(jnp.bfloat16).reshape(sel_rows, top_count, slot_count)
    token_pick = jnp.sum(route_pick, axis=1)
    reward = lax.psum(jnp.dot(chosen, reward_w, preferred_element_type=jnp.float32), "tensor")
    keep_scale = jax.nn.sigmoid(reward)
    slot_scale = slot_factor(route_hit, keep_scale[:, None] * gates)
    token_send = jnp.einsum(
        "sp,sd->pd", token_pick, chosen, preferred_element_type=jnp.float32
    ).astype(jnp.bfloat16)
    picked_target = jnp.einsum("sp,sd->pd", token_pick, target, preferred_element_type=jnp.float32)
    cot_send = (picked_target * slot_scale[:, None]).astype(jnp.bfloat16)
    token_part, cot_part = (
        lax.all_to_all(token_send, "dp", split_axis=0, concat_axis=0, tiled=True),
        lax.all_to_all(cot_send, "dp", split_axis=0, concat_axis=0, tiled=True),
    )
    received_tokens, received_cots = (
        lax.all_gather(token_part, "tensor", axis=1, tiled=True),
        lax.all_gather(cot_part, "tensor", axis=1, tiled=True),
    )
    width = received_tokens.shape[1]
    token_rows = received_tokens.reshape(owners, exp_dev, capacity, width)
    cot_rows = received_cots.reshape(owners, exp_dev, capacity, width)
    gate_act = jnp.einsum("secd,efd->secf", token_rows, w_gate, preferred_element_type=jnp.float32)
    up_act = jnp.einsum("secd,efd->secf", token_rows, w_up, preferred_element_type=jnp.float32)
    sigmoid_gate = jax.nn.sigmoid(gate_act)
    hidden = (gate_act * sigmoid_gate * up_act).astype(jnp.bfloat16)
    partial_value = jnp.einsum("secf,efd->secd", hidden, w_down, preferred_element_type=jnp.float32)
    summed = lax.psum_scatter(
        partial_value.astype(jnp.bfloat16), "tensor", scatter_dimension=3, tiled=True
    )
    returned = lax.all_to_all(summed, "dp", split_axis=0, concat_axis=0, tiled=True).reshape(
        slot_count, -1
    )
    route_rows = jnp.einsum("skp,pd->skd", route_pick, returned, preferred_element_type=jnp.float32)
    mixed = jnp.sum(route_rows * gates[:, :, None], axis=1).astype(jnp.bfloat16)
    hidden_grad = jnp.einsum("secd,efd->secf", cot_rows, w_down, preferred_element_type=jnp.float32)
    gate_grad = (
        hidden_grad * up_act * sigmoid_gate * (1.0 + gate_act * (1.0 - sigmoid_gate))
    ).astype(jnp.bfloat16)
    up_grad = (hidden_grad * gate_act * sigmoid_gate).astype(jnp.bfloat16)
    grad_down = jnp.einsum(
        "secf,secd->efd", hidden, cot_rows, preferred_element_type=jnp.float32
    ).astype(jnp.bfloat16)
    grad_gate = jnp.einsum(
        "secf,secd->efd", gate_grad, token_rows, preferred_element_type=jnp.float32
    ).astype(jnp.bfloat16)
    grad_up = jnp.einsum(
        "secf,secd->efd", up_grad, token_rows, preferred_element_type=jnp.float32
    ).astype(jnp.bfloat16)
    return (mixed, grad_gate, grad_up, grad_down)


def place():
    d = lax.axis_index("dp")
    c = lax.axis_index("tensor")
    z, q = d // PLANE, d % PLANE
    y, x = q // 2, q % 2
    mates = [((y + ry) % 2) * 2 + (x + rx) % 2 for ry, rx in ((0, 1), (1, 0), (1, 1))]
    return d, c, z, q, mates


def greet(d, c, z, q, mates):
    barrier = pltpu.get_barrier_semaphore()
    for m in mates:
        pl.semaphore_signal(barrier, inc=1, device_id=(z * PLANE + m, c), device_id_type=MESH)
    pl.semaphore_signal(barrier, inc=1, device_id=(d, 1 - c), device_id_type=MESH)

    @pl.when(z > 0)
    def _():
        pl.semaphore_signal(barrier, inc=1, device_id=(d - PLANE, c), device_id_type=MESH)

    @pl.when(z < LINE - 1)
    def _():
        pl.semaphore_signal(barrier, inc=1, device_id=(d + PLANE, c), device_id_type=MESH)


def greeted(z):
    below, above = (z + LINE - 1) // LINE, (2 * LINE - 2 - z) // LINE
    pl.semaphore_wait(pltpu.get_barrier_semaphore(), 4 + below + above)


def remote(src, dst, send, recv, dev):
    return pltpu.make_async_remote_copy(
        src_ref=src, dst_ref=dst, send_sem=send, recv_sem=recv, device_id=dev, device_id_type=MESH
    )


def sigmoid(v):
    return 1.0 / (1.0 + jnp.exp(-v))


def chunks(capacity):
    ends = [(j + 1) * capacity // 16 * 16 for j in range(LINE - 1)]
    ends.append(-(-LINE * capacity // 16) * 16)
    offs = [0] + ends[:-1]
    return offs, [b - a for a, b in zip(offs, ends)]


def layer_kernel(
    capacity, pad, pool_hbm, sel_ref, rw_ref, rt_ref, gt_ref, target_hbm, wg_hbm, wu_hbm, wd_hbm,
    mixed_ref, gg_ref, gu_ref, gd_ref,
    pool_ref, rt_vmem, gt_vmem, tok, cot, gate_act, up_act, hid, ggrad, ugrad, val,
    data, side_ref, scale, part, part_in, stage,
    partner_in, back, plane_in, acc, out_stage, line_in,
    lsem, zsend, zrecv, ssend, srecv, csend, crecv, xsend, xrecv, tsend, trecv, psend, precv,
    vsend, vrecv, bsend, brecv, usend, urecv,
):
    d, c, z, q, mates = place()
    experts = LINE * PLANE
    sel_rows, half = mixed_ref.shape
    top = gt_ref.shape[0]
    wg, wu, wd = gg_ref.at[0], gu_ref.at[0], gd_ref.at[0]
    units, width = wg.shape
    span = PLANE * pad
    offs, sizes = chunks(capacity)
    rows = (tok, cot)
    mine = pl.ds(pl.multiple_of(c * half, half), half)
    other = pl.ds(pl.multiple_of((1 - c) * half, half), half)
    partner = (d, 1 - c)
    seq = (z, z + 1 - 2 * (z % 2), 2 - z // 2, 3 - 3 * (z // 2))
    piece = half // PARTS
    nt = (((1,), (1,)), ((), ()))
    tn = (((0,), (0,)), ((), ()))

    greet(d, c, z, q, mates)
    loads = [
        pltpu.make_async_copy(src, dst, lsem.at[i])
        for i, (src, dst) in enumerate((
            (pool_hbm, pool_ref), (target_hbm, data.at[1, z]), (wg_hbm.at[0], wg),
            (wu_hbm.at[0], wu), (wd_hbm.at[0], wd), (rt_ref, rt_vmem), (gt_ref, gt_vmem),
        ))
    ]
    for i in (5, 6, 0, 1, 2, 3, 4):
        loads[i].start()

    for j in range(LINE):
        if sizes[j] < pad:
            for a in (0, 1):
                rows[a][j, :, sizes[j] : pad, :] = jnp.zeros(
                    (PLANE, pad - sizes[j], width), BF16
                )
    loads[5].wait()
    loads[6].wait()
    expert_id = lax.broadcasted_iota(jnp.int32, (experts, sel_rows), 0)
    member = jnp.zeros((experts, sel_rows), F32)
    gate = jnp.zeros((experts, sel_rows), F32)
    for k in range(top):
        eq = rt_vmem[k : k + 1, :] == expert_id
        member = member + jnp.where(eq, 1.0, 0.0)
        gate = gate + jnp.where(eq, gt_vmem[k : k + 1, :], 0.0)
    tri = jnp.where(
        lax.broadcasted_iota(jnp.int32, (sel_rows, sel_rows), 0)
        < lax.broadcasted_iota(jnp.int32, (sel_rows, sel_rows), 1),
        1.0,
        0.0,
    ).astype(BF16)
    before = jnp.dot(member.astype(BF16), tri, preferred_element_type=F32)
    side_ref[z, 0:experts, :] = jnp.where(member > 0.5, before, -1024.0)
    side_ref[z, experts : 2 * experts, :] = gate

    pool_rows = pool_ref.shape[0]
    hit = (
        lax.broadcasted_iota(jnp.int32, (pool_rows, sel_rows), 0) == sel_ref[...] - d * pool_rows
    ).astype(F32).astype(BF16)
    loads[0].wait()
    chosen = lax.dot_general(
        hit, pool_ref[...], tn, preferred_element_type=F32
    ).astype(BF16)
    data[0, z] = chosen
    rw = rw_ref[...].astype(F32)
    rw_rows = jnp.concatenate(
        [jnp.broadcast_to(rw[i : i + 1, :], (16, rw.shape[1])) for i in range(rw.shape[0])],
        axis=1,
    ).astype(BF16)
    part[...] = lax.dot_general(rw_rows, chosen, nt, preferred_element_type=F32)

    def zcopy(a, s, way, kind):
        blk = z - way * s
        dev = (d + way * PLANE, c)
        w = (way + 1) // 2
        if kind == 1:
            spot = data.at[a, blk]
            return remote(spot, spot, zsend.at[a, w, s], zrecv.at[a, blk], dev)
        if a == 0:
            spot = side_ref.at[blk]
            return remote(spot, spot, ssend.at[w, s], srecv.at[blk], dev)
        spot = scale.at[blk]
        return remote(spot, spot, csend.at[w, s], crecv.at[blk], dev)

    def sends(s, way):
        blk, to = z - way * s, z + way
        return (blk >= 0) & (blk < LINE) & (to >= 0) & (to < LINE)

    def zstart(a, s, which=(0, 1)):
        for way in (1, -1):
            @pl.when(sends(s, way))
            def _():
                for i in which:
                    zcopy(a, s, way, i).start()

    def arrives(s, way):
        blk = z - way * (s + 1)
        return (blk >= 0) & (blk < LINE)

    def zwait(a, s):
        for way in (1, -1):
            @pl.when(arrives(s, way))
            def _():
                blk = z - way * (s + 1)
                remote(
                    data.at[a, blk], data.at[a, blk], zsend.at[a, 0, 0], zrecv.at[a, blk], partner
                ).wait_recv()
                if a == 0:
                    remote(
                        side_ref.at[blk], side_ref.at[blk], ssend.at[0, 0], srecv.at[blk], partner
                    ).wait_recv()
                else:
                    remote(
                        scale.at[blk], scale.at[blk], csend.at[0, 0], crecv.at[blk], partner
                    ).wait_recv()

    def tcopy(a, j, m):
        spot = rows[a].at[j, m, 0 : sizes[j], mine]
        return remote(spot, spot, tsend.at[a, j, m], trecv.at[a, j, m], partner)

    def tarrive(a, j):
        for m in range(PLANE):
            spot = rows[a].at[j, m, 0 : sizes[j], other]
            remote(spot, spot, tsend.at[a, j, m], trecv.at[a, j, m], partner).wait_recv()

    def xcopy(a, j, r):
        return remote(
            stage.at[a, j, r, 0 : sizes[j], :],
            rows[a].at[j, q, 0 : sizes[j], mine],
            xsend.at[a, j, r],
            xrecv.at[a, j, q],
            (z * PLANE + mates[r], c),
        )

    slot_id = lax.broadcasted_iota(jnp.int32, (pad, sel_rows), 0).astype(F32)

    def pick(a, j):
        size = sizes[j]
        sources = [(seq[i], float(offs[j] - capacity * i)) for i in ((j, j - 1) if j else (j,))]
        sides = (2, 0, 1, 3)
        hits, factors = [], []
        for r in sides:
            e = z * PLANE + (mates[r] if r < 3 else q)
            ms = [slot_id[:size] + base == side_ref[b, pl.ds(e, 1), :] for b, base in sources]
            hits.append(jnp.concatenate([jnp.where(m, 1.0, 0.0) for m in ms], axis=1))
            if a == 1:
                total = sum(
                    jnp.where(m, scale[b, pl.ds(e, 1), :], 0.0) for m, (b, _) in zip(ms, sources)
                )
                factors.append(jnp.sum(total, axis=1, keepdims=True))
        hits = jnp.concatenate(hits, axis=0).astype(BF16)
        if a == 1:
            factors = jnp.concatenate(factors, axis=0)
        cut = 256 if half % 256 == 0 else half
        for n in range(half // cut):
            cols = pl.ds(n * cut, cut)
            source = jnp.concatenate([data[a, b, :, cols] for b, _ in sources], axis=0)
            picked = jnp.dot(hits, source, preferred_element_type=F32)
            if a == 1:
                picked = picked * factors
            picked = picked.astype(BF16)
            for i, r in enumerate(sides):
                got = picked[i * size : (i + 1) * size]
                if r < 3:
                    stage[a, j, r, 0:size, cols] = got
                else:
                    spot = pl.ds(pl.multiple_of(c * half + n * cut, cut), cut)
                    rows[a][j, q, 0:size, spot] = got
        for r in (2, 0, 1):
            xcopy(a, j, r).start()
        tcopy(a, j, q).start()

    def forward(a, j):
        for r in (0, 1, 2):
            m = mates[r]
            remote(
                stage.at[a, j, r, 0 : sizes[j], :], rows[a].at[j, m, 0 : sizes[j], mine],
                xsend.at[a, j, r], xrecv.at[a, j, m], partner,
            ).wait_recv()
            tcopy(a, j, m).start()

    def vcopy(j):
        return remote(
            val.at[j, :, 0 : sizes[j], other], partner_in.at[j, :, 0 : sizes[j], :],
            vsend.at[j], vrecv.at[j], partner,
        )

    tile = 512 if half % 512 == 0 else half

    def group(j):
        lanes = pl.ds(j * span, span)
        tarrive(0, j)
        x = tok[j].reshape(span, width)
        g = lax.dot_general(wg[...], x, nt, preferred_element_type=F32)
        u = lax.dot_general(wu[...], x, nt, preferred_element_type=F32)
        gate_act[j] = g
        up_act[j] = u
        h = (g * sigmoid(g) * u).astype(BF16)
        hid[:, lanes] = h
        for side in (1 - c, c):
            for n in range(half // tile):
                cols = pl.ds(pl.multiple_of(side * half + n * tile, tile), tile)
                v = lax.dot_general(h, wd[:, cols], tn, preferred_element_type=F32)
                val[j, :, :, cols] = v.astype(BF16).reshape(PLANE, pad, tile)
            if side is not c:
                vcopy(j).start()

    def grad_group(j):
        lanes = pl.ds(j * span, span)
        tarrive(1, j)
        x = cot[j].reshape(span, width)
        hg = lax.dot_general(wd[...], x, nt, preferred_element_type=F32)
        g = gate_act[j]
        s = sigmoid(g)
        ggrad[:, lanes] = (hg * up_act[j] * s * (1.0 + g * (1.0 - s))).astype(BF16)
        ugrad[:, lanes] = (hg * g * s).astype(BF16)

    grads = ((ggrad, tok, wg), (ugrad, tok, wu), (hid, cot, wd))
    strip = 256 if width % 256 == 0 else width
    strips = width // strip

    def grad_strip(n, carry):
        cols = pl.ds(pl.multiple_of(n * strip, strip), strip)
        for left, right, out in grads:
            r = right[:, :, :, cols].reshape(experts * pad, strip)
            out[:, cols] = jnp.dot(left[...], r, preferred_element_type=F32).astype(BF16)
        return carry

    def bcopy(j, r, h):
        cols = pl.ds(h * piece, piece)
        return remote(
            back.at[j, r, 0 : sizes[j], cols], plane_in.at[j, q, 0 : sizes[j], cols],
            bsend.at[j, r, h], brecv.at[j, q, h],
            (z * PLANE + mates[r], c),
        )

    def give(j):
        size = sizes[j]
        vcopy(j).wait_recv()
        for h in range(PARTS):
            cols = pl.ds(h * piece, piece)
            spot = pl.ds(pl.multiple_of(c * half + h * piece, piece), piece)
            for r in (2, 0, 1, 3):
                m = mates[r] if r < 3 else q
                total = (
                    val[j, m, 0:size, spot].astype(F32) + partner_in[j, m, 0:size, cols].astype(F32)
                ).astype(BF16)
                if r < 3:
                    back[j, r, 0:size, cols] = total
                    bcopy(j, r, h).start()
                else:
                    plane_in[j, q, 0:size, cols] = total

    def combine(j):
        blk = seq[j]
        weights, takes = [], []
        for m in range(PLANE):
            e = z * PLANE + m
            rank = side_ref[blk, pl.ds(e, 1), :]
            strength = side_ref[blk, pl.ds(experts + e, 1), :]
            spots = [(j, sizes[j])] + ([(j + 1, 16)] if j + 1 < LINE else [])
            for i, size in spots:
                base = float(offs[i] - capacity * j)
                w = jnp.where(slot_id[:size] + base == rank, strength, 0.0)
                high = w.astype(BF16)
                weights += [high, (w - high.astype(F32)).astype(BF16)]
                takes += [(i, m, size)] * 2
        weights = jnp.concatenate(weights, axis=0)
        for h in range(PARTS):
            cols = pl.ds(h * piece, piece)
            for r in range(3):
                remote(
                    back.at[j, r, 0 : sizes[j], cols], plane_in.at[j, mates[r], 0 : sizes[j], cols],
                    bsend.at[j, r, h], brecv.at[j, mates[r], h], partner,
                ).wait_recv()
            values = jnp.concatenate(
                [plane_in[i, m, 0:size, cols] for i, m, size in takes], axis=0
            )
            acc[blk, :, cols] = lax.dot_general(weights, values, tn, preferred_element_type=F32)

    def ucopy(w, s, h):
        cols = pl.ds(h * piece, piece)
        to = d + (2 * w - 1) * PLANE
        return remote(
            out_stage.at[w, s, :, cols], line_in.at[w, s, :, cols], usend.at[w, s, h],
            urecv.at[w, s, h], (to, c),
        )

    def height(w):
        return z if w == 1 else LINE - 1 - z

    def lifts(w, s):
        return (height(w) <= s) & (height(w) < LINE - 1)

    def lands(w, s):
        return (height(w) > 0) & (height(w) - 1 <= s)

    def lift(s):
        for w in (1, 0):
            blk = z + (2 * w - 1) * (LINE - 1 - s)
            for h in range(PARTS):
                cols = pl.ds(h * piece, piece)
                if s > 0:
                    @pl.when(lands(w, s - 1))
                    def _():
                        ucopy(w, s - 1, h).wait_recv()

                    @pl.when(lifts(w, s) & (height(w) > 0))
                    def _():
                        out_stage[w, s, :, cols] = (
                            acc[blk, :, cols] + line_in[w, s - 1, :, cols].astype(F32)
                        ).astype(BF16)
                        ucopy(w, s, h).start()

                @pl.when(lifts(w, s) & (height(w) == 0))
                def _():
                    out_stage[w, s, :, cols] = acc[blk, :, cols].astype(BF16)
                    ucopy(w, s, h).start()

    greeted(z)
    reward_copy = remote(part, part_in, psend, precv, partner)
    reward_copy.start()
    zstart(0, 0)
    pick(0, 0)
    loads[1].wait()
    zstart(1, 0, (1,))
    reward_copy.wait()
    scale[z] = sigmoid(part[0:1, :] + part_in[0:1, :]) * side_ref[z, experts : 2 * experts, :]
    zstart(1, 0, (0,))
    pick(1, 0)
    forward(0, 0)
    zwait(0, 0)
    zstart(0, 1)
    pick(0, 1)
    for cp in loads[2:5]:
        cp.wait()
    group(0)
    forward(1, 0)
    zwait(1, 0)
    pick(1, 1)
    grad_group(0)
    forward(0, 1)
    zwait(0, 1)
    zstart(0, 2)
    zstart(1, 1)
    pick(0, 2)
    group(1)
    forward(1, 1)
    zwait(0, 2)
    pick(0, 3)
    grad_group(1)
    forward(0, 2)
    zwait(1, 1)
    zstart(1, 2)
    pick(1, 2)
    group(2)
    forward(0, 3)
    zwait(1, 2)
    pick(1, 3)
    group(3)
    for j in (3, 2, 1, 0):
        give(j)
    forward(1, 2)
    grad_group(2)
    forward(1, 3)
    grad_group(3)

    last = LINE - 2
    done = 0
    for s in range(LINE - 1):
        upto = strips * (s + 1) // (LINE - 1)
        combine(LINE - 1 - s)
        lift(s)
        lax.fori_loop(done, upto, grad_strip, 0)
        done = upto
    combine(0)
    for h in range(PARTS):
        cols = pl.ds(h * piece, piece)
        for w in (1, 0):
            @pl.when(lands(w, last))
            def _():
                ucopy(w, last, h).wait_recv()
                acc[z, :, cols] = acc[z, :, cols] + line_in[w, last, :, cols].astype(F32)
        mixed_ref[:, cols] = acc[z, :, cols].astype(BF16)

    for j in range(LINE):
        vcopy(j).wait_send()
        for a in (0, 1):
            for m in range(PLANE):
                tcopy(a, j, m).wait_send()
        for r in range(3):
            for h in range(PARTS):
                bcopy(j, r, h).wait_send()
            for a in (0, 1):
                xcopy(a, j, r).wait_send()
    for s in range(LINE - 1):
        for w in (1, 0):
            @pl.when(lifts(w, s))
            def _():
                for h in range(PARTS):
                    ucopy(w, s, h).wait_send()

        for a in (0, 1):
            for way in (1, -1):
                @pl.when(sends(s, way))
                def _():
                    for kind in (0, 1):
                        zcopy(a, s, way, kind).wait_send()


def flush_kernel(*refs):
    count = len(refs) // 2
    sem = refs[-1]
    copies = []
    for i in range(count):
        src, dst = refs[i], refs[count + i]
        for j in range(PARTS):
            cut = pl.ds(j * (src.shape[-2] // PARTS), src.shape[-2] // PARTS)
            at = (cut,) if len(src.shape) == 2 else (0, cut)
            copies.append(pltpu.make_async_copy(src.at[at], dst.at[at], sem.at[i, j]))
    for cp in copies:
        cp.start()
    for cp in copies:
        cp.wait()


def flush(*outs):
    return pl.pallas_call(
        flush_kernel,
        name="flush",
        out_shape=tuple(jax.ShapeDtypeStruct(o.shape, o.dtype) for o in outs),
        in_specs=vmem(len(outs)),
        out_specs=tuple(hbm(len(outs))),
        scratch_shapes=[DMA((len(outs), PARTS))],
        compiler_params=pltpu.CompilerParams(vmem_limit_bytes=1 << 20),
    )(*[pltpu.with_memory_space_constraint(o, pltpu.VMEM) for o in outs])


def vmem(count):
    return [pl.BlockSpec(memory_space=pltpu.VMEM)] * count


def hbm(count):
    return [pl.BlockSpec(memory_space=pl.ANY)] * count


DMA = pltpu.SemaphoreType.DMA


def planar(pool, select, reward_w, routes, gates, target, w_gate, w_up, w_down):
    experts = LINE * PLANE
    sel_rows, top = routes.shape
    capacity = 5 * sel_rows * top // (4 * experts)
    pad = max(chunks(capacity)[1])
    half = target.shape[1]
    units, width = w_gate.shape[1:]
    span = PLANE * pad
    grad_shape = pltpu.VMEM(w_gate.shape, BF16)
    rw = reward_w.reshape(half // 128, 128)
    slots = pltpu.VMEM((LINE, PLANE, pad, width), BF16)
    act = pltpu.VMEM((LINE, units, span), F32)
    flat = pltpu.VMEM((units, experts * pad), BF16)
    outs = pl.pallas_call(
        functools.partial(layer_kernel, capacity, pad),
        name="layer",
        out_shape=(pltpu.VMEM((sel_rows, half), BF16), grad_shape, grad_shape, grad_shape),
        in_specs=hbm(1) + vmem(2) + hbm(6),
        out_specs=tuple(vmem(4)),
        scratch_shapes=[
            pltpu.VMEM(pool.shape, BF16), pltpu.VMEM((top, sel_rows), jnp.int32),
            pltpu.VMEM((top, sel_rows), F32), slots, slots, act, act, flat, flat, flat, slots,
            pltpu.VMEM((2, LINE, sel_rows, half), BF16),
            pltpu.VMEM((LINE, 2 * experts, sel_rows), F32),
            pltpu.VMEM((LINE, experts, sel_rows), F32),
            pltpu.VMEM((16, sel_rows), F32),
            pltpu.VMEM((16, sel_rows), F32),
            pltpu.VMEM((2, LINE, 3, pad, half), BF16),
            pltpu.VMEM((LINE, PLANE, pad, half), BF16),
            pltpu.VMEM((LINE, 3, pad, half), BF16),
            pltpu.VMEM((LINE, PLANE, pad, half), BF16),
            pltpu.VMEM((LINE, sel_rows, half), F32),
            pltpu.VMEM((2, LINE - 1, sel_rows, half), BF16),
            pltpu.VMEM((2, LINE - 1, sel_rows, half), BF16),
            DMA((7,)),
            DMA((2, 2, LINE)), DMA((2, LINE)), DMA((2, LINE)), DMA((LINE,)),
            DMA((2, LINE)), DMA((LINE,)), DMA((2, LINE, 3)), DMA((2, LINE, PLANE)),
            DMA((2, LINE, PLANE)), DMA((2, LINE, PLANE)), DMA, DMA,
            DMA((LINE,)), DMA((LINE,)), DMA((LINE, 3, PARTS)), DMA((LINE, PLANE, PARTS)),
            DMA((2, LINE, PARTS)), DMA((2, LINE, PARTS)),
        ],
        compiler_params=pltpu.CompilerParams(
            collective_id=0, has_side_effects=True, vmem_limit_bytes=57 * 10**6
        ),
    )(pool, select.reshape(1, sel_rows), rw, routes.T, gates.T, target,
      w_gate, w_up, w_down)
    return flush(*outs)


def solution(mesh):
    in_specs = (
        P("dp", "tensor"), P("dp"), P("tensor"), P("dp", None), P("dp", None), P("dp", "tensor"),
        P("dp", "tensor", None), P("dp", "tensor", None), P("dp", "tensor", None),
    )
    out_specs = (
        P("dp", "tensor"), P("dp", "tensor", None), P("dp", "tensor", None),
        P("dp", "tensor", None),
    )
    dp, tensor = mesh.shape["dp"], mesh.shape["tensor"]
    fits = tensor == 2 and dp == LINE * PLANE
    local = planar if fits else generic
    return jax.shard_map(local, mesh=mesh, in_specs=in_specs, out_specs=out_specs, check_vma=False)
```

time: 100 us -> 81.9 us (0.82)
  Pallas kernels: 92.8 us -> 80.9 us
  local copies, waits for them, and re-layouts: 6.74 us -> 0 us
    pallas_call x1 -> x2, Pallas kernels: 92.8 us -> 80.9 us  [the longest x1 77.4 us: planar(): pl.pallas_call(functools.partial(layer_kernel, capacity, pad), name='laye...]
    unnamed x4 -> x0, local copies, waits for them, and re-layouts: 5.44 us -> none
    broadcast_in_dim x1 -> x0, local copies, waits for them, and re-layouts: 1.3 us -> none  [planar(): rw = jnp.broadcast_to(reward_w[None, :], (16, half))]
where the time goes in v1:
time: 81.9 us; the launch traced here: 81.7 us
  Pallas kernels  80.9 us (99%)
    pallas_call x1, Pallas kernels, planar(): pl.pallas_call(functools.partial(layer_kernel, capacity, pad), name='laye...  77.4 us
    pallas_call x1, Pallas kernels, flush(): pl.pallas_call(flush_kernel, name='flush', out_shape=tuple((jax.ShapeDtyp...  3.55 us

profile of v1, /device:TPU:0, one launch (start us, length us, event | category | flops | bytes accessed | tf_op | source)
XLA Modules:
  0.0 81.7 jit_solution(3089004748432469686)
XLA Ops:
  0.6 77.4 %layer.1 = (bf16[128,1024]{1,0:T(8,128)(2,1)S(1)}, bf16[1,704,2048]{2,1,0:T(8,128)(2,1)S(1)}, bf16[1,704,2048]{2,1,0:T(8,128)(2,1)S(1)}, bf16[1,704,2048]{2,1,0:T(8,128)(2,1)S(1)}) custom-call(bf16[256,1024]{1,0:T(8,128)(2,1)} %pool_hbm.1, s32[1,128]{1,0:T(1,128)} %bitcast.7, bf16[8,128]{1,0:T(8,128)(2,1)} %bitcast.6, s32[6,128]{1,0:T(8,128)} %bitcast.4, ...), custom_call_target="tpu_custom_call" | custom-call | tf_op jit(solution)/shard_map/layer/pallas_call | solution.py:605
  78.0 3.5 %flush.1 = (bf16[128,1024]{1,0:T(8,128)(2,1)}, bf16[1,704,2048]{2,1,0:T(8,128)(2,1)}, bf16[1,704,2048]{2,1,0:T(8,128)(2,1)}, bf16[1,704,2048]{2,1,0:T(8,128)(2,1)}) custom-call(bf16[128,1024]{1,0:T(8,128)(2,1)S(1)} %get-tuple-element.8.refs_0_, bf16[1,704,2048]{2,1,0:T(8,128)(2,1)S(1)} %get-tuple-element.9.refs_1_, ...), custom_call_target="tpu_custom_call" | custom-call | tf_op jit(solution)/shard_map/flush/pallas_call | solution.py:570

commit v2 on v1

--- a/solution.py
+++ b/solution.py
@@ -134,9 +134,9 @@
 
 
 def layer_kernel(
-    capacity, pad, pool_hbm, sel_ref, rw_ref, rt_ref, gt_ref, target_hbm, wg_hbm, wu_hbm, wd_hbm,
-    mixed_ref, gg_ref, gu_ref, gd_ref,
-    pool_ref, rt_vmem, gt_vmem, tok, cot, gate_act, up_act, hid, ggrad, ugrad, val,
+    capacity, pad, pool_hbm, sel_hbm, rw_hbm, rt_hbm, gt_hbm, target_hbm, wg_hbm, wu_hbm, wd_hbm,
+    mixed_ref, gg_ref, gu_ref, gd_ref, tok, cot, hid, ggrad, ugrad,
+    pool_ref, sel_ref, rw_ref, rt_ref, gt_ref, gate_act, up_act, val,
     data, side_ref, scale, part, part_in, stage,
     partner_in, back, plane_in, acc, out_stage, line_in,
     lsem, zsend, zrecv, ssend, srecv, csend, crecv, xsend, xrecv, tsend, trecv, psend, precv,
@@ -145,7 +145,7 @@
     d, c, z, q, mates = place()
     experts = LINE * PLANE
     sel_rows, half = mixed_ref.shape
-    top = gt_ref.shape[0]
+    top = gt_hbm.shape[0]
     wg, wu, wd = gg_ref.at[0], gu_ref.at[0], gd_ref.at[0]
     units, width = wg.shape
     span = PLANE * pad
@@ -163,53 +163,24 @@
     loads = [
         pltpu.make_async_copy(src, dst, lsem.at[i])
         for i, (src, dst) in enumerate((
-            (pool_hbm, pool_ref), (target_hbm, data.at[1, z]), (wg_hbm.at[0], wg),
-            (wu_hbm.at[0], wu), (wd_hbm.at[0], wd), (rt_ref, rt_vmem), (gt_ref, gt_vmem),
+            (sel_hbm, sel_ref), (pool_hbm, pool_ref), (rt_hbm, rt_ref), (gt_hbm, gt_ref),
+            (rw_hbm, rw_ref), (target_hbm, data.at[1, z]), (wg_hbm.at[0], wg), (wu_hbm.at[0], wu),
+            (wd_hbm.at[0], wd),
         ))
     ]
-    for i in (5, 6, 0, 1, 2, 3, 4):
-        loads[i].start()
-
-    for j in range(LINE):
-        if sizes[j] < pad:
-            for a in (0, 1):
-                rows[a][j, :, sizes[j] : pad, :] = jnp.zeros(
-                    (PLANE, pad - sizes[j], width), BF16
-                )
-    loads[5].wait()
-    loads[6].wait()
-    expert_id = lax.broadcasted_iota(jnp.int32, (experts, sel_rows), 0)
-    member = jnp.zeros((experts, sel_rows), F32)
-    gate = jnp.zeros((experts, sel_rows), F32)
-    for k in range(top):
-        eq = rt_vmem[k : k + 1, :] == expert_id
-        member = member + jnp.where(eq, 1.0, 0.0)
-        gate = gate + jnp.where(eq, gt_vmem[k : k + 1, :], 0.0)
-    tri = jnp.where(
-        lax.broadcasted_iota(jnp.int32, (sel_rows, sel_rows), 0)
-        < lax.broadcasted_iota(jnp.int32, (sel_rows, sel_rows), 1),
-        1.0,
-        0.0,
-    ).astype(BF16)
-    before = jnp.dot(member.astype(BF16), tri, preferred_element_type=F32)
-    side_ref[z, 0:experts, :] = jnp.where(member > 0.5, before, -1024.0)
-    side_ref[z, experts : 2 * experts, :] = gate
-
+    for cp in loads:
+        cp.start()
+
+    loads[0].wait()
     pool_rows = pool_ref.shape[0]
     hit = (
         lax.broadcasted_iota(jnp.int32, (pool_rows, sel_rows), 0) == sel_ref[...] - d * pool_rows
     ).astype(F32).astype(BF16)
-    loads[0].wait()
+    loads[1].wait()
     chosen = lax.dot_general(
         hit, pool_ref[...], tn, preferred_element_type=F32
     ).astype(BF16)
     data[0, z] = chosen
-    rw = rw_ref[...].astype(F32)
-    rw_rows = jnp.concatenate(
-        [jnp.broadcast_to(rw[i : i + 1, :], (16, rw.shape[1])) for i in range(rw.shape[0])],
-        axis=1,
-    ).astype(BF16)
-    part[...] = lax.dot_general(rw_rows, chosen, nt, preferred_element_type=F32)
 
     def zcopy(a, s, way, kind):
         blk = z - way * s
@@ -217,12 +188,12 @@
         w = (way + 1) // 2
         if kind == 1:
             spot = data.at[a, blk]
-            return remote(spot, spot, zsend.at[a, w, s], zrecv.at[a, blk], dev)
+            return remote(spot, spot, zsend.at[w], zrecv.at[a, blk], dev)
         if a == 0:
             spot = side_ref.at[blk]
-            return remote(spot, spot, ssend.at[w, s], srecv.at[blk], dev)
+            return remote(spot, spot, ssend.at[w], srecv.at[blk], dev)
         spot = scale.at[blk]
-        return remote(spot, spot, csend.at[w, s], crecv.at[blk], dev)
+        return remote(spot, spot, csend.at[w], crecv.at[blk], dev)
 
     def sends(s, way):
         blk, to = z - way * s, z + way
@@ -245,32 +216,34 @@
             def _():
                 blk = z - way * (s + 1)
                 remote(
-                    data.at[a, blk], data.at[a, blk], zsend.at[a, 0, 0], zrecv.at[a, blk], partner
+                    data.at[a, blk], data.at[a, blk], zsend.at[0], zrecv.at[a, blk], partner
                 ).wait_recv()
                 if a == 0:
                     remote(
-                        side_ref.at[blk], side_ref.at[blk], ssend.at[0, 0], srecv.at[blk], partner
+                        side_ref.at[blk], side_ref.at[blk], ssend.at[0], srecv.at[blk], partner
                     ).wait_recv()
                 else:
                     remote(
-                        scale.at[blk], scale.at[blk], csend.at[0, 0], crecv.at[blk], partner
+                        scale.at[blk], scale.at[blk], csend.at[0], crecv.at[blk], partner
                     ).wait_recv()
 
     def tcopy(a, j, m):
         spot = rows[a].at[j, m, 0 : sizes[j], mine]
-        return remote(spot, spot, tsend.at[a, j, m], trecv.at[a, j, m], partner)
+        return remote(spot, spot, tsend.at[a, min(j, 1)], trecv.at[a, j], partner)
+
+    def tall(a, j, side):
+        spot = rows[a].at[j, :, 0 : sizes[j], side]
+        return remote(spot, spot, tsend.at[a, min(j, 1)], trecv.at[a, j], partner)
 
     def tarrive(a, j):
-        for m in range(PLANE):
-            spot = rows[a].at[j, m, 0 : sizes[j], other]
-            remote(spot, spot, tsend.at[a, j, m], trecv.at[a, j, m], partner).wait_recv()
+        tall(a, j, other).wait_recv()
 
     def xcopy(a, j, r):
         return remote(
             stage.at[a, j, r, 0 : sizes[j], :],
             rows[a].at[j, q, 0 : sizes[j], mine],
-            xsend.at[a, j, r],
-            xrecv.at[a, j, q],
+            xsend.at[min(j, 1)],
+            xrecv.at[a, j],
             (z * PLANE + mates[r], c),
         )
 
@@ -313,18 +286,17 @@
         tcopy(a, j, q).start()
 
     def forward(a, j):
-        for r in (0, 1, 2):
-            m = mates[r]
-            remote(
-                stage.at[a, j, r, 0 : sizes[j], :], rows[a].at[j, m, 0 : sizes[j], mine],
-                xsend.at[a, j, r], xrecv.at[a, j, m], partner,
-            ).wait_recv()
+        remote(
+            stage.at[a, j, :, 0 : sizes[j], :], rows[a].at[j, 0:3, 0 : sizes[j], mine],
+            xsend.at[min(j, 1)], xrecv.at[a, j], partner,
+        ).wait_recv()
+        for m in mates:
             tcopy(a, j, m).start()
 
     def vcopy(j):
         return remote(
             val.at[j, :, 0 : sizes[j], other], partner_in.at[j, :, 0 : sizes[j], :],
-            vsend.at[j], vrecv.at[j], partner,
+            vsend.at[min(j, 1)], vrecv.at[j], partner,
         )
 
     tile = 512 if half % 512 == 0 else half
@@ -359,7 +331,7 @@
 
     grads = ((ggrad, tok, wg), (ugrad, tok, wu), (hid, cot, wd))
     strip = 256 if width % 256 == 0 else width
-    strips = width // strip
+    strips = width // strip - left_over(width // strip)
 
     def grad_strip(n, carry):
         cols = pl.ds(pl.multiple_of(n * strip, strip), strip)
@@ -372,7 +344,7 @@
         cols = pl.ds(h * piece, piece)
         return remote(
             back.at[j, r, 0 : sizes[j], cols], plane_in.at[j, q, 0 : sizes[j], cols],
-            bsend.at[j, r, h], brecv.at[j, q, h],
+            bsend.at[min(j, 1)], brecv.at[j, h],
             (z * PLANE + mates[r], c),
         )
 
@@ -393,7 +365,7 @@
                 else:
                     plane_in[j, q, 0:size, cols] = total
 
-    def combine(j):
+    def mixing(j):
         blk = seq[j]
         weights, takes = [], []
         for m in range(PLANE):
@@ -407,24 +379,23 @@
                 high = w.astype(BF16)
                 weights += [high, (w - high.astype(F32)).astype(BF16)]
                 takes += [(i, m, size)] * 2
-        weights = jnp.concatenate(weights, axis=0)
-        for h in range(PARTS):
-            cols = pl.ds(h * piece, piece)
-            for r in range(3):
-                remote(
-                    back.at[j, r, 0 : sizes[j], cols], plane_in.at[j, mates[r], 0 : sizes[j], cols],
-                    bsend.at[j, r, h], brecv.at[j, mates[r], h], partner,
-                ).wait_recv()
-            values = jnp.concatenate(
-                [plane_in[i, m, 0:size, cols] for i, m, size in takes], axis=0
-            )
-            acc[blk, :, cols] = lax.dot_general(weights, values, tn, preferred_element_type=F32)
+        return jnp.concatenate(weights, axis=0), takes
+
+    def combine(j, h, mix):
+        weights, takes = mix
+        cols = pl.ds(h * piece, piece)
+        remote(
+            back.at[j, :, 0 : sizes[j], cols], plane_in.at[j, 0:3, 0 : sizes[j], cols],
+            bsend.at[min(j, 1)], brecv.at[j, h], partner,
+        ).wait_recv()
+        values = jnp.concatenate([plane_in[i, m, 0:size, cols] for i, m, size in takes], axis=0)
+        acc[seq[j], :, cols] = lax.dot_general(weights, values, tn, preferred_element_type=F32)
 
     def ucopy(w, s, h):
         cols = pl.ds(h * piece, piece)
         to = d + (2 * w - 1) * PLANE
         return remote(
-            out_stage.at[w, s, :, cols], line_in.at[w, s, :, cols], usend.at[w, s, h],
+            out_stage.at[w, s, :, cols], line_in.at[w, s, :, cols], usend.at[w],
             urecv.at[w, s, h], (to, c),
         )
 
@@ -437,35 +408,72 @@
     def lands(w, s):
         return (height(w) > 0) & (height(w) - 1 <= s)
 
-    def lift(s):
+    def lift(s, h):
+        cols = pl.ds(h * piece, piece)
         for w in (1, 0):
             blk = z + (2 * w - 1) * (LINE - 1 - s)
-            for h in range(PARTS):
-                cols = pl.ds(h * piece, piece)
-                if s > 0:
-                    @pl.when(lands(w, s - 1))
-                    def _():
-                        ucopy(w, s - 1, h).wait_recv()
-
-                    @pl.when(lifts(w, s) & (height(w) > 0))
-                    def _():
-                        out_stage[w, s, :, cols] = (
-                            acc[blk, :, cols] + line_in[w, s - 1, :, cols].astype(F32)
-                        ).astype(BF16)
-                        ucopy(w, s, h).start()
-
-                @pl.when(lifts(w, s) & (height(w) == 0))
+            if s > 0:
+                @pl.when(lands(w, s - 1))
                 def _():
-                    out_stage[w, s, :, cols] = acc[blk, :, cols].astype(BF16)
+                    ucopy(w, s - 1, h).wait_recv()
+
+                @pl.when(lifts(w, s) & (height(w) > 0))
+                def _():
+                    out_stage[w, s, :, cols] = (
+                        acc[blk, :, cols] + line_in[w, s - 1, :, cols].astype(F32)
+                    ).astype(BF16)
                     ucopy(w, s, h).start()
 
+            @pl.when(lifts(w, s) & (height(w) == 0))
+            def _():
+                out_stage[w, s, :, cols] = acc[blk, :, cols].astype(BF16)
+                ucopy(w, s, h).start()
+
+    def sides():
+        expert_id = lax.broadcasted_iota(jnp.int32, (experts, sel_rows), 0)
+        member = jnp.zeros((experts, sel_rows), F32)
+        gate = jnp.zeros((experts, sel_rows), F32)
+        for k in range(top):
+            eq = rt_ref[k : k + 1, :] == expert_id
+            member = member + jnp.where(eq, 1.0, 0.0)
+            gate = gate + jnp.where(eq, gt_ref[k : k + 1, :], 0.0)
+        tri = jnp.where(
+            lax.broadcasted_iota(jnp.int32, (sel_rows, sel_rows), 0)
+            < lax.broadcasted_iota(jnp.int32, (sel_rows, sel_rows), 1),
+            1.0,
+            0.0,
+        ).astype(BF16)
+        before = jnp.dot(member.astype(BF16), tri, preferred_element_type=F32)
+        side_ref[z, 0:experts, :] = jnp.where(member > 0.5, before, -1024.0)
+        side_ref[z, experts : 2 * experts, :] = gate
+
+    def rewards():
+        rw = rw_ref[...].astype(F32)
+        rw_rows = jnp.concatenate(
+            [jnp.broadcast_to(rw[i : i + 1, :], (16, rw.shape[1])) for i in range(rw.shape[0])],
+            axis=1,
+        ).astype(BF16)
+        part[...] = lax.dot_general(rw_rows, data[0, z], nt, preferred_element_type=F32)
+
+    reward_copy = remote(part, part_in, psend, precv, partner)
     greeted(z)
-    reward_copy = remote(part, part_in, psend, precv, partner)
+    zstart(0, 0, (1,))
+    loads[2].wait()
+    loads[3].wait()
+    sides()
+    zstart(0, 0, (0,))
+    loads[5].wait()
+    zstart(1, 0, (1,))
+    pick(0, 0)
+    loads[4].wait()
+    rewards()
     reward_copy.start()
-    zstart(0, 0)
-    pick(0, 0)
-    loads[1].wait()
-    zstart(1, 0, (1,))
+    for j in range(LINE):
+        if sizes[j] < pad:
+            for a in (0, 1):
+                rows[a][j, :, sizes[j] : pad, :] = jnp.zeros(
+                    (PLANE, pad - sizes[j], width), BF16
+                )
     reward_copy.wait()
     scale[z] = sigmoid(part[0:1, :] + part_in[0:1, :]) * side_ref[z, experts : 2 * experts, :]
     zstart(1, 0, (0,))
@@ -474,7 +482,7 @@
     zwait(0, 0)
     zstart(0, 1)
     pick(0, 1)
-    for cp in loads[2:5]:
+    for cp in loads[6:9]:
         cp.wait()
     group(0)
     forward(1, 0)
@@ -508,15 +516,42 @@
     grad_group(3)
 
     last = LINE - 2
-    done = 0
+    turns = (LINE - 1) * PARTS
+    done, turn = 0, 0
     for s in range(LINE - 1):
-        upto = strips * (s + 1) // (LINE - 1)
-        combine(LINE - 1 - s)
-        lift(s)
-        lax.fori_loop(done, upto, grad_strip, 0)
-        done = upto
-    combine(0)
+        j = LINE - 1 - s
+        mix = mixing(j)
+        for h in range(PARTS):
+            combine(j, h, mix)
+            lift(s, h)
+            upto = strips * turn // (turns - 2)
+            upto = min(upto, strips)
+            if upto > done:
+                lax.fori_loop(done, upto, grad_strip, 0)
+                done = upto
+            turn = turn + 1
+    lax.fori_loop(done, strips, grad_strip, 0)
+
+    def sent(src, sem):
+        remote(src, src, sem, vrecv.at[0], partner).wait_send()
+
+    for w in (0, 1):
+        for n in range(1, LINE):
+            @pl.when(LINE - height(1 - w) == n)
+            def _():
+                sent(data.at[:, 0:n], zsend.at[w])
+                sent(side_ref.at[0:n], ssend.at[w])
+                sent(scale.at[0:n], csend.at[w])
+    for i, cut in ((0, slice(0, 1)), (1, slice(1, LINE))):
+        size = sizes[0] if i == 0 else pad
+        sent(stage.at[:, cut, :, 0:size, :], xsend.at[i])
+        sent(val.at[cut, :, 0:size, other], vsend.at[i])
+        for a in (0, 1):
+            sent(rows[a].at[cut, :, 0:size, mine], tsend.at[a, i])
+
+    mix = mixing(0)
     for h in range(PARTS):
+        combine(0, h, mix)
         cols = pl.ds(h * piece, piece)
         for w in (1, 0):
             @pl.when(lands(w, last))
@@ -525,56 +560,59 @@
                 acc[z, :, cols] = acc[z, :, cols] + line_in[w, last, :, cols].astype(F32)
         mixed_ref[:, cols] = acc[z, :, cols].astype(BF16)
 
-    for j in range(LINE):
-        vcopy(j).wait_send()
-        for a in (0, 1):
-            for m in range(PLANE):
-                tcopy(a, j, m).wait_send()
-        for r in range(3):
-            for h in range(PARTS):
-                bcopy(j, r, h).wait_send()
-            for a in (0, 1):
-                xcopy(a, j, r).wait_send()
-    for s in range(LINE - 1):
-        for w in (1, 0):
-            @pl.when(lifts(w, s))
+    for w in (0, 1):
+        for n in range(1, LINE):
+            @pl.when(LINE - 1 - height(w) == n)
             def _():
-                for h in range(PARTS):
-                    ucopy(w, s, h).wait_send()
-
-        for a in (0, 1):
-            for way in (1, -1):
-                @pl.when(sends(s, way))
-                def _():
-                    for kind in (0, 1):
-                        zcopy(a, s, way, kind).wait_send()
-
-
-def flush_kernel(*refs):
-    count = len(refs) // 2
-    sem = refs[-1]
-    copies = []
-    for i in range(count):
-        src, dst = refs[i], refs[count + i]
-        for j in range(PARTS):
-            cut = pl.ds(j * (src.shape[-2] // PARTS), src.shape[-2] // PARTS)
-            at = (cut,) if len(src.shape) == 2 else (0, cut)
-            copies.append(pltpu.make_async_copy(src.at[at], dst.at[at], sem.at[i, j]))
+                sent(out_stage.at[w, 0:n], usend.at[w])
+    sent(back.at[0:1, :, 0 : sizes[0], :], bsend.at[0])
+    sent(back.at[1:LINE], bsend.at[1])
+
+
+def left_over(strips):
+    return strips // 4
+
+
+def flush_kernel(
+    mixed, gg, gu, gd, tok, cot, hid, ggrad, ugrad, mixed_out, gg_out, gu_out, gd_out, last, sem
+):
+    units, width = gg.shape[1:]
+    late = last.shape[1] * last.shape[3]
+    strip = last.shape[3]
+    early = width - late
+    rows = units // PARTS
+    copies = [pltpu.make_async_copy(mixed, mixed_out, sem.at[0, 0])]
+    grads = ((gg, gg_out, ggrad, tok), (gu, gu_out, ugrad, tok), (gd, gd_out, hid, cot))
+    for i, (src, dst, _, _) in enumerate(grads):
+        for p in range(PARTS):
+            at = (0, pl.ds(p * rows, rows), pl.ds(0, early))
+            copies.append(pltpu.make_async_copy(src.at[at], dst.at[at], sem.at[i + 1, p]))
     for cp in copies:
         cp.start()
+    for n in range(last.shape[1]):
+        cols = pl.ds(early + n * strip, strip)
+        for i, (_, dst, left, right) in enumerate(grads):
+            r = right[:, :, :, cols].reshape(left.shape[1], strip)
+            last[i, n] = jnp.dot(left[...], r, preferred_element_type=F32).astype(BF16)
+            cp = pltpu.make_async_copy(last.at[i, n], dst.at[0, :, cols], sem.at[i + 1, PARTS + n])
+            cp.start()
+            copies.append(cp)
     for cp in copies:
         cp.wait()
 
 
 def flush(*outs):
+    units, width = outs[1].shape[1:]
+    strip = 256 if width % 256 == 0 else width
+    late = left_over(width // strip)
     return pl.pallas_call(
         flush_kernel,
         name="flush",
-        out_shape=tuple(jax.ShapeDtypeStruct(o.shape, o.dtype) for o in outs),
+        out_shape=tuple(jax.ShapeDtypeStruct(o.shape, o.dtype) for o in outs[:4]),
         in_specs=vmem(len(outs)),
-        out_specs=tuple(hbm(len(outs))),
-        scratch_shapes=[DMA((len(outs), PARTS))],
-        compiler_params=pltpu.CompilerParams(vmem_limit_bytes=1 << 20),
+        out_specs=tuple(hbm(4)),
+        scratch_shapes=[pltpu.VMEM((3, late, units, strip), BF16), DMA((4, PARTS + late))],
+        compiler_params=pltpu.CompilerParams(vmem_limit_bytes=12 << 20),
     )(*[pltpu.with_memory_space_constraint(o, pltpu.VMEM) for o in outs])
 
 
@@ -605,12 +643,16 @@
     outs = pl.pallas_call(
         functools.partial(layer_kernel, capacity, pad),
         name="layer",
-        out_shape=(pltpu.VMEM((sel_rows, half), BF16), grad_shape, grad_shape, grad_shape),
-        in_specs=hbm(1) + vmem(2) + hbm(6),
-        out_specs=tuple(vmem(4)),
+        out_shape=(
+            pltpu.VMEM((sel_rows, half), BF16), grad_shape, grad_shape, grad_shape,
+            slots, slots, flat, flat, flat,
+        ),
+        in_specs=hbm(9),
+        out_specs=tuple(vmem(9)),
         scratch_shapes=[
-            pltpu.VMEM(pool.shape, BF16), pltpu.VMEM((top, sel_rows), jnp.int32),
-            pltpu.VMEM((top, sel_rows), F32), slots, slots, act, act, flat, flat, flat, slots,
+            pltpu.VMEM(pool.shape, BF16), pltpu.VMEM((1, sel_rows), jnp.int32),
+            pltpu.VMEM(rw.shape, BF16), pltpu.VMEM((top, sel_rows), jnp.int32),
+            pltpu.VMEM((top, sel_rows), F32), act, act, slots,
             pltpu.VMEM((2, LINE, sel_rows, half), BF16),
             pltpu.VMEM((LINE, 2 * experts, sel_rows), F32),
             pltpu.VMEM((LINE, experts, sel_rows), F32),
@@ -623,15 +665,15 @@
             pltpu.VMEM((LINE, sel_rows, half), F32),
             pltpu.VMEM((2, LINE - 1, sel_rows, half), BF16),
             pltpu.VMEM((2, LINE - 1, sel_rows, half), BF16),
-            DMA((7,)),
-            DMA((2, 2, LINE)), DMA((2, LINE)), DMA((2, LINE)), DMA((LINE,)),
-            DMA((2, LINE)), DMA((LINE,)), DMA((2, LINE, 3)), DMA((2, LINE, PLANE)),
-            DMA((2, LINE, PLANE)), DMA((2, LINE, PLANE)), DMA, DMA,
-            DMA((LINE,)), DMA((LINE,)), DMA((LINE, 3, PARTS)), DMA((LINE, PLANE, PARTS)),
-            DMA((2, LINE, PARTS)), DMA((2, LINE, PARTS)),
+            DMA((9,)),
+            DMA((2,)), DMA((2, LINE)), DMA((2,)), DMA((LINE,)),
+            DMA((2,)), DMA((LINE,)), DMA((2,)), DMA((2, LINE)),
+            DMA((2, 2)), DMA((2, LINE)), DMA, DMA,
+            DMA((2,)), DMA((LINE,)), DMA((2,)), DMA((LINE, PARTS)),
+            DMA((2,)), DMA((2, LINE - 1, PARTS)),
         ],
         compiler_params=pltpu.CompilerParams(
-            collective_id=0, has_side_effects=True, vmem_limit_bytes=57 * 10**6
+            collective_id=0, has_side_effects=True, vmem_limit_bytes=44 * 10**6
         ),
     )(pool, select.reshape(1, sel_rows), rw, routes.T, gates.T, target,
       w_gate, w_up, w_down)

time: 81.9 us -> 78.6 us (0.960)
  Pallas kernels: 80.9 us -> 77.7 us
    pallas_call x1, Pallas kernels: 77.4 us -> 74.1 us  [planar(): pl.pallas_call(functools.partial(layer_kernel, capacity, pad), name='laye...]
where the time goes in v2:
time: 78.6 us; the launch traced here: 78.5 us
  Pallas kernels  77.7 us (99%)
  between operations  0.8 us (1%)
    pallas_call x1, Pallas kernels, planar(): pl.pallas_call(functools.partial(layer_kernel, capacity, pad), name='laye...  74.1 us
    pallas_call x1, Pallas kernels, flush(): pl.pallas_call(flush_kernel, name='flush', out_shape=tuple((jax.ShapeDtyp...  3.58 us

profile of v2, /device:TPU:0, one launch (start us, length us, event | category | flops | bytes accessed | tf_op | source)
XLA Modules:
  0.0 78.5 jit_solution(15449788451016434163)
XLA Ops:
  0.6 74.1 %layer.1 = (bf16[128,1024]{1,0:T(8,128)(2,1)S(1)}, bf16[1,704,2048]{2,1,0:T(8,128)(2,1)S(1)}, bf16[1,704,2048]{2,1,0:T(8,128)(2,1)S(1)}, bf16[1,704,2048]{2,1,0:...) custom-call(bf16[256,1024]{1,0:T(8,128)(2,1)} %pool_hbm.1, ...), custom_call_target="tpu_custom_call" | custom-call | tf_op jit(solution)/shard_map/layer/pallas_call | solution.py:643
  74.7 3.6 %flush.1 = (bf16[128,1024]{1,0:T(8,128)(2,1)}, bf16[1,704,2048]{2,1,0:T(8,128)(2,1)}, bf16[1,704,2048]{2,1,0:T(8,128)(2,1)}, bf16[1,704,2048]{2,1,0:T(8,128)(2,1)}) custom-call(bf16[128,1024]{1,0:T(8,128)(2,1)S(1)} %get-tuple-element.13.mixed, bf16[1,704,2048]{2,1,0:T(8,128)(2,1)S(1)} %get-tuple-element.14.gg, ...), custom_call_target="tpu_custom_call" | custom-call | tf_op jit(solution)/shard_map/flush/pallas_call | solution.py:608

commit v3 on v2

--- a/solution.py
+++ b/solution.py
@@ -168,7 +168,7 @@
             (wd_hbm.at[0], wd),
         ))
     ]
-    for cp in loads:
+    for cp in loads[:5]:
         cp.start()
 
     loads[0].wait()
@@ -177,6 +177,7 @@
         lax.broadcasted_iota(jnp.int32, (pool_rows, sel_rows), 0) == sel_ref[...] - d * pool_rows
     ).astype(F32).astype(BF16)
     loads[1].wait()
+    loads[5].start()
     chosen = lax.dot_general(
         hit, pool_ref[...], tn, preferred_element_type=F32
     ).astype(BF16)
@@ -195,13 +196,19 @@
         spot = scale.at[blk]
         return remote(spot, spot, csend.at[w], crecv.at[blk], dev)
 
+    def inside(to):
+        return (z > 0) & (z < LINE - 1) & (to > 0) & (to < LINE - 1)
+
+    def among(links, to):
+        return {"all": True, "inner": inside(to), "outer": jnp.logical_not(inside(to))}[links]
+
     def sends(s, way):
         blk, to = z - way * s, z + way
         return (blk >= 0) & (blk < LINE) & (to >= 0) & (to < LINE)
 
-    def zstart(a, s, which=(0, 1)):
+    def zstart(a, s, which=(0, 1), links="all"):
         for way in (1, -1):
-            @pl.when(sends(s, way))
+            @pl.when(sends(s, way) & among(links, z + way))
             def _():
                 for i in which:
                     zcopy(a, s, way, i).start()
@@ -210,9 +217,9 @@
         blk = z - way * (s + 1)
         return (blk >= 0) & (blk < LINE)
 
-    def zwait(a, s):
+    def zwait(a, s, links="all"):
         for way in (1, -1):
-            @pl.when(arrives(s, way))
+            @pl.when(arrives(s, way) & among(links, z - way))
             def _():
                 blk = z - way * (s + 1)
                 remote(
@@ -458,12 +465,14 @@
     reward_copy = remote(part, part_in, psend, precv, partner)
     greeted(z)
     zstart(0, 0, (1,))
+    for cp in loads[6:9]:
+        cp.start()
     loads[2].wait()
     loads[3].wait()
     sides()
     zstart(0, 0, (0,))
     loads[5].wait()
-    zstart(1, 0, (1,))
+    zstart(1, 0, (1,), "outer")
     pick(0, 0)
     loads[4].wait()
     rewards()
@@ -481,21 +490,24 @@
     forward(0, 0)
     zwait(0, 0)
     zstart(0, 1)
+    zstart(1, 0, (1,), "inner")
     pick(0, 1)
     for cp in loads[6:9]:
         cp.wait()
     group(0)
     forward(1, 0)
-    zwait(1, 0)
+    zwait(1, 0, "outer")
     pick(1, 1)
     grad_group(0)
     forward(0, 1)
     zwait(0, 1)
     zstart(0, 2)
-    zstart(1, 1)
+    zstart(1, 1, links="inner")
     pick(0, 2)
     group(1)
     forward(1, 1)
+    zwait(1, 0, "inner")
+    zstart(1, 1, links="outer")
     zwait(0, 2)
     pick(0, 3)
     grad_group(1)

time: 78.6 us -> 77 us (0.980)
  Pallas kernels: 77.7 us -> 76 us
    pallas_call x1, Pallas kernels: 74.1 us -> 72.5 us  [planar(): pl.pallas_call(functools.partial(layer_kernel, capacity, pad), name='laye...]
where the time goes in v3:
time: 77 us; the launch traced here: 76.9 us
  Pallas kernels  76 us (99%)
  between operations  0.8 us (1%)
    pallas_call x1, Pallas kernels, planar(): pl.pallas_call(functools.partial(layer_kernel, capacity, pad), name='laye...  72.5 us
    pallas_call x1, Pallas kernels, flush(): pl.pallas_call(flush_kernel, name='flush', out_shape=tuple((jax.ShapeDtyp...  3.58 us

profile of v3, /device:TPU:0, one launch (start us, length us, event | category | flops | bytes accessed | tf_op | source)
XLA Modules:
  0.0 76.9 jit_solution(1676146108780828679)
XLA Ops:
  0.6 72.5 %layer.1 = (bf16[128,1024]{1,0:T(8,128)(2,1)S(1)}, bf16[1,704,2048]{2,1,0:T(8,128)(2,1)S(1)}, bf16[1,704,2048]{2,1,0:T(8,128)(2,1)S(1)}, bf16[1,704,2048]{2,1,0:...) custom-call(bf16[256,1024]{1,0:T(8,128)(2,1)} %pool_hbm.1, ...), custom_call_target="tpu_custom_call" | custom-call | tf_op jit(solution)/shard_map/layer/pallas_call | solution.py:655
  73.1 3.6 %flush.1 = (bf16[128,1024]{1,0:T(8,128)(2,1)}, bf16[1,704,2048]{2,1,0:T(8,128)(2,1)}, bf16[1,704,2048]{2,1,0:T(8,128)(2,1)}, bf16[1,704,2048]{2,1,0:T(8,128)(2,1)}) custom-call(bf16[128,1024]{1,0:T(8,128)(2,1)S(1)} %get-tuple-element.13.mixed, bf16[1,704,2048]{2,1,0:T(8,128)(2,1)S(1)} %get-tuple-element.14.gg, ...), custom_call_target="tpu_custom_call" | custom-call | tf_op jit(solution)/shard_map/flush/pallas_call | solution.py:620

commit v4 on v3

--- a/solution.py
+++ b/solution.py
@@ -168,14 +168,35 @@
             (wd_hbm.at[0], wd),
         ))
     ]
-    for cp in loads[:5]:
-        cp.start()
+    for i in (0, 2, 3, 1, 4):
+        loads[i].start()
+
+    def sides():
+        expert_id = lax.broadcasted_iota(jnp.int32, (experts, sel_rows), 0)
+        member = jnp.zeros((experts, sel_rows), F32)
+        gate = jnp.zeros((experts, sel_rows), F32)
+        for k in range(top):
+            eq = rt_ref[k : k + 1, :] == expert_id
+            member = member + jnp.where(eq, 1.0, 0.0)
+            gate = gate + jnp.where(eq, gt_ref[k : k + 1, :], 0.0)
+        tri = jnp.where(
+            lax.broadcasted_iota(jnp.int32, (sel_rows, sel_rows), 0)
+            < lax.broadcasted_iota(jnp.int32, (sel_rows, sel_rows), 1),
+            1.0,
+            0.0,
+        ).astype(BF16)
+        before = jnp.dot(member.astype(BF16), tri, preferred_element_type=F32)
+        side_ref[z, 0:experts, :] = jnp.where(member > 0.5, before, -1024.0)
+        side_ref[z, experts : 2 * experts, :] = gate
 
     loads[0].wait()
     pool_rows = pool_ref.shape[0]
     hit = (
         lax.broadcasted_iota(jnp.int32, (pool_rows, sel_rows), 0) == sel_ref[...] - d * pool_rows
     ).astype(F32).astype(BF16)
+    loads[2].wait()
+    loads[3].wait()
+    sides()
     loads[1].wait()
     loads[5].start()
     chosen = lax.dot_general(
@@ -436,24 +457,6 @@
                 out_stage[w, s, :, cols] = acc[blk, :, cols].astype(BF16)
                 ucopy(w, s, h).start()
 
-    def sides():
-        expert_id = lax.broadcasted_iota(jnp.int32, (experts, sel_rows), 0)
-        member = jnp.zeros((experts, sel_rows), F32)
-        gate = jnp.zeros((experts, sel_rows), F32)
-        for k in range(top):
-            eq = rt_ref[k : k + 1, :] == expert_id
-            member = member + jnp.where(eq, 1.0, 0.0)
-            gate = gate + jnp.where(eq, gt_ref[k : k + 1, :], 0.0)
-        tri = jnp.where(
-            lax.broadcasted_iota(jnp.int32, (sel_rows, sel_rows), 0)
-            < lax.broadcasted_iota(jnp.int32, (sel_rows, sel_rows), 1),
-            1.0,
-            0.0,
-        ).astype(BF16)
-        before = jnp.dot(member.astype(BF16), tri, preferred_element_type=F32)
-        side_ref[z, 0:experts, :] = jnp.where(member > 0.5, before, -1024.0)
-        side_ref[z, experts : 2 * experts, :] = gate
-
     def rewards():
         rw = rw_ref[...].astype(F32)
         rw_rows = jnp.concatenate(
@@ -465,15 +468,12 @@
     reward_copy = remote(part, part_in, psend, precv, partner)
     greeted(z)
     zstart(0, 0, (1,))
+    zstart(0, 0, (0,))
+    pick(0, 0)
+    loads[5].wait()
+    zstart(1, 0, (1,), "outer")
     for cp in loads[6:9]:
         cp.start()
-    loads[2].wait()
-    loads[3].wait()
-    sides()
-    zstart(0, 0, (0,))
-    loads[5].wait()
-    zstart(1, 0, (1,), "outer")
-    pick(0, 0)
     loads[4].wait()
     rewards()
     reward_copy.start()
@@ -528,7 +528,6 @@
     grad_group(3)
 
     last = LINE - 2
-    turns = (LINE - 1) * PARTS
     done, turn = 0, 0
     for s in range(LINE - 1):
         j = LINE - 1 - s
@@ -536,8 +535,7 @@
         for h in range(PARTS):
             combine(j, h, mix)
             lift(s, h)
-            upto = strips * turn // (turns - 2)
-            upto = min(upto, strips)
+            upto = min(2 * turn + 1, strips)
             if upto > done:
                 lax.fori_loop(done, upto, grad_strip, 0)
                 done = upto

time: 77 us -> 76.3 us (level)
  no operation moved by 1% of the time
where the time goes in v4:
time: 76.3 us; the launch traced here: 76.2 us
  Pallas kernels  75.4 us (99%)
  between operations  0.8 us (1%)
    pallas_call x1, Pallas kernels, planar(): pl.pallas_call(functools.partial(layer_kernel, capacity, pad), name='laye...  71.8 us
    pallas_call x1, Pallas kernels, flush(): pl.pallas_call(flush_kernel, name='flush', out_shape=tuple((jax.ShapeDtyp...  3.58 us

profile of v4, /device:TPU:0, one launch (start us, length us, event | category | flops | bytes accessed | tf_op | source)
XLA Modules:
  0.0 76.2 jit_solution(11203627241372144908)
XLA Ops:
  0.6 71.8 %layer.1 = (bf16[128,1024]{1,0:T(8,128)(2,1)S(1)}, bf16[1,704,2048]{2,1,0:T(8,128)(2,1)S(1)}, bf16[1,704,2048]{2,1,0:T(8,128)(2,1)S(1)}, bf16[1,704,2048]{2,1,0:...) custom-call(bf16[256,1024]{1,0:T(8,128)(2,1)} %pool_hbm.1, ...), custom_call_target="tpu_custom_call" | custom-call | tf_op jit(solution)/shard_map/layer/pallas_call | solution.py:653
  72.5 3.6 %flush.1 = (bf16[128,1024]{1,0:T(8,128)(2,1)}, bf16[1,704,2048]{2,1,0:T(8,128)(2,1)}, bf16[1,704,2048]{2,1,0:T(8,128)(2,1)}, bf16[1,704,2048]{2,1,0:T(8,128)(2,1)}) custom-call(bf16[128,1024]{1,0:T(8,128)(2,1)S(1)} %get-tuple-element.13.mixed, bf16[1,704,2048]{2,1,0:T(8,128)(2,1)S(1)} %get-tuple-element.14.gg, ...), custom_call_target="tpu_custom_call" | custom-call | tf_op jit(solution)/shard_map/flush/pallas_call | solution.py:618

commit v5 on v4

--- a/solution.py
+++ b/solution.py
@@ -10,6 +10,7 @@
 PLANE = 4
 LINE = 4
 PARTS = 2
+CUTS = 1
 F32 = jnp.float32
 BF16 = jnp.bfloat16
 
@@ -140,7 +141,7 @@
     data, side_ref, scale, part, part_in, stage,
     partner_in, back, plane_in, acc, out_stage, line_in,
     lsem, zsend, zrecv, ssend, srecv, csend, crecv, xsend, xrecv, tsend, trecv, psend, precv,
-    vsend, vrecv, bsend, brecv, usend, urecv,
+    vsend, vrecv, bsend, brecv, usend, urecv, gsend, grecv,
 ):
     d, c, z, q, mates = place()
     experts = LINE * PLANE
@@ -168,7 +169,7 @@
             (wd_hbm.at[0], wd),
         ))
     ]
-    for i in (0, 2, 3, 1, 4):
+    for i in (1, 0, 2, 3, 4):
         loads[i].start()
 
     def sides():
@@ -194,9 +195,6 @@
     hit = (
         lax.broadcasted_iota(jnp.int32, (pool_rows, sel_rows), 0) == sel_ref[...] - d * pool_rows
     ).astype(F32).astype(BF16)
-    loads[2].wait()
-    loads[3].wait()
-    sides()
     loads[1].wait()
     loads[5].start()
     chosen = lax.dot_general(
@@ -212,8 +210,11 @@
             spot = data.at[a, blk]
             return remote(spot, spot, zsend.at[w], zrecv.at[a, blk], dev)
         if a == 0:
-            spot = side_ref.at[blk]
+            spot = side_ref.at[blk, 0:experts]
             return remote(spot, spot, ssend.at[w], srecv.at[blk], dev)
+        if kind == 2:
+            spot = side_ref.at[blk, experts : 2 * experts]
+            return remote(spot, spot, gsend.at[w], grecv.at[blk], dev)
         spot = scale.at[blk]
         return remote(spot, spot, csend.at[w], crecv.at[blk], dev)
 
@@ -247,13 +248,20 @@
                     data.at[a, blk], data.at[a, blk], zsend.at[0], zrecv.at[a, blk], partner
                 ).wait_recv()
                 if a == 0:
-                    remote(
-                        side_ref.at[blk], side_ref.at[blk], ssend.at[0], srecv.at[blk], partner
-                    ).wait_recv()
+                    spot = side_ref.at[blk, 0:experts]
+                    remote(spot, spot, ssend.at[0], srecv.at[blk], partner).wait_recv()
                 else:
                     remote(
                         scale.at[blk], scale.at[blk], csend.at[0], crecv.at[blk], partner
                     ).wait_recv()
+
+    def gates_wait(s):
+        for way in (1, -1):
+            @pl.when(arrives(s, way))
+            def _():
+                blk = z - way * (s + 1)
+                spot = side_ref.at[blk, experts : 2 * experts]
+                remote(spot, spot, gsend.at[0], grecv.at[blk], partner).wait_recv()
 
     def tcopy(a, j, m):
         spot = rows[a].at[j, m, 0 : sizes[j], mine]
@@ -468,6 +476,9 @@
     reward_copy = remote(part, part_in, psend, precv, partner)
     greeted(z)
     zstart(0, 0, (1,))
+    loads[2].wait()
+    loads[3].wait()
+    sides()
     zstart(0, 0, (0,))
     pick(0, 0)
     loads[5].wait()
@@ -514,18 +525,24 @@
     forward(0, 2)
     zwait(1, 1)
     zstart(1, 2)
+    zstart(1, 0, (2,))
     pick(1, 2)
     group(2)
     forward(0, 3)
     zwait(1, 2)
     pick(1, 3)
+    gates_wait(0)
+    zstart(1, 1, (2,))
     group(3)
     for j in (3, 2, 1, 0):
         give(j)
     forward(1, 2)
+    gates_wait(1)
+    zstart(1, 2, (2,))
     grad_group(2)
     forward(1, 3)
     grad_group(3)
+    gates_wait(2)
 
     last = LINE - 2
     done, turn = 0, 0
@@ -550,7 +567,8 @@
             @pl.when(LINE - height(1 - w) == n)
             def _():
                 sent(data.at[:, 0:n], zsend.at[w])
-                sent(side_ref.at[0:n], ssend.at[w])
+                sent(side_ref.at[0:n, 0:experts], ssend.at[w])
+                sent(side_ref.at[0:n, experts : 2 * experts], gsend.at[w])
                 sent(scale.at[0:n], csend.at[w])
     for i, cut in ((0, slice(0, 1)), (1, slice(1, LINE))):
         size = sizes[0] if i == 0 else pad
@@ -590,11 +608,11 @@
     late = last.shape[1] * last.shape[3]
     strip = last.shape[3]
     early = width - late
-    rows = units // PARTS
+    rows = units // CUTS
     copies = [pltpu.make_async_copy(mixed, mixed_out, sem.at[0, 0])]
     grads = ((gg, gg_out, ggrad, tok), (gu, gu_out, ugrad, tok), (gd, gd_out, hid, cot))
     for i, (src, dst, _, _) in enumerate(grads):
-        for p in range(PARTS):
+        for p in range(CUTS):
             at = (0, pl.ds(p * rows, rows), pl.ds(0, early))
             copies.append(pltpu.make_async_copy(src.at[at], dst.at[at], sem.at[i + 1, p]))
     for cp in copies:
@@ -604,7 +622,7 @@
         for i, (_, dst, left, right) in enumerate(grads):
             r = right[:, :, :, cols].reshape(left.shape[1], strip)
             last[i, n] = jnp.dot(left[...], r, preferred_element_type=F32).astype(BF16)
-            cp = pltpu.make_async_copy(last.at[i, n], dst.at[0, :, cols], sem.at[i + 1, PARTS + n])
+            cp = pltpu.make_async_copy(last.at[i, n], dst.at[0, :, cols], sem.at[i + 1, CUTS + n])
             cp.start()
             copies.append(cp)
     for cp in copies:
@@ -621,7 +639,7 @@
         out_shape=tuple(jax.ShapeDtypeStruct(o.shape, o.dtype) for o in outs[:4]),
         in_specs=vmem(len(outs)),
         out_specs=tuple(hbm(4)),
-        scratch_shapes=[pltpu.VMEM((3, late, units, strip), BF16), DMA((4, PARTS + late))],
+        scratch_shapes=[pltpu.VMEM((3, late, units, strip), BF16), DMA((4, CUTS + late))],
         compiler_params=pltpu.CompilerParams(vmem_limit_bytes=12 << 20),
     )(*[pltpu.with_memory_space_constraint(o, pltpu.VMEM) for o in outs])
 
@@ -680,7 +698,7 @@
             DMA((2,)), DMA((LINE,)), DMA((2,)), DMA((2, LINE)),
             DMA((2, 2)), DMA((2, LINE)), DMA, DMA,
             DMA((2,)), DMA((LINE,)), DMA((2,)), DMA((LINE, PARTS)),
-            DMA((2,)), DMA((2, LINE - 1, PARTS)),
+            DMA((2,)), DMA((2, LINE - 1, PARTS)), DMA((2,)), DMA((LINE,)),
         ],
         compiler_params=pltpu.CompilerParams(
             collective_id=0, has_side_effects=True, vmem_limit_bytes=44 * 10**6

time: 76.3 us -> 76.2 us (level)
  no operation moved by 1% of the time
where the time goes in v5:
time: 76.2 us; the launch traced here: 76.1 us
  Pallas kernels  75.3 us (99%)
  between operations  0.8 us (1%)
    pallas_call x1, Pallas kernels, planar(): pl.pallas_call(functools.partial(layer_kernel, capacity, pad), name='laye...  71.7 us
    pallas_call x1, Pallas kernels, flush(): pl.pallas_call(flush_kernel, name='flush', out_shape=tuple((jax.ShapeDtyp...  3.54 us

profile of v5, /device:TPU:0, one launch (start us, length us, event | category | flops | bytes accessed | tf_op | source)
XLA Modules:
  0.0 76.1 jit_solution(14547415150284456289)
XLA Ops:
  0.6 71.7 %layer.1 = (bf16[128,1024]{1,0:T(8,128)(2,1)S(1)}, bf16[1,704,2048]{2,1,0:T(8,128)(2,1)S(1)}, bf16[1,704,2048]{2,1,0:T(8,128)(2,1)S(1)}, bf16[1,704,2048]{2,1,0:...) custom-call(bf16[256,1024]{1,0:T(8,128)(2,1)} %pool_hbm.1, ...), custom_call_target="tpu_custom_call" | custom-call | tf_op jit(solution)/shard_map/layer/pallas_call | solution.py:671
  72.4 3.5 %flush.1 = (bf16[128,1024]{1,0:T(8,128)(2,1)}, bf16[1,704,2048]{2,1,0:T(8,128)(2,1)}, bf16[1,704,2048]{2,1,0:T(8,128)(2,1)}, bf16[1,704,2048]{2,1,0:T(8,128)(2,1)}) custom-call(bf16[128,1024]{1,0:T(8,128)(2,1)S(1)} %get-tuple-element.13.mixed, bf16[1,704,2048]{2,1,0:T(8,128)(2,1)S(1)} %get-tuple-element.14.gg, ...), custom_call_target="tpu_custom_call" | custom-call | tf_op jit(solution)/shard_map/flush/pallas_call | solution.py:636
